TPU v7x, 768 devices: a whole 4x8x12 slice. The times are simulated.
768 devices in a mesh: outer: 8 (over y), rep: 12 (over z_hi, x), mp: 8 (over z_lo, core).
Axes of the slice: x: 4, y: 8, z: 12 (z_hi: 3, z_lo: 4; z = z_hi * 4 + z_lo), core: 2. Of those that a mesh axis runs over, the one named last changes fastest.
Arguments:
- deltas: bfloat16 [8, 12, 768, 14336], P('outer', 'rep', None, 'mp'), may hold values from -6 to 6
- pod_momentum: float32 [8, 768, 14336], P('outer', 'rep', 'mp'), may hold values from -6 to 6
- global_momentum: float32 [12, 64, 14336], P('rep', 'outer', 'mp'), may hold values from -6 to 6
- master: float32 [12, 64, 14336], P('rep', 'outer', 'mp'), may hold values from -6 to 6
Outputs:
- params_new: bfloat16 [768, 14336], P(None, 'mp')
- pod_momentum_new: float32 [8, 768, 14336], P('outer', 'rep', 'mp')
- global_momentum_new: float32 [12, 64, 14336], P('rep', 'outer', 'mp')
All inputs are finite; a program needn't handle non-finite values.
Results may differ from a plain program's by a relative error of at most 0.011.
Values may be sent and summed in bfloat16 or wider, within the bound.
No kernel may reach another device: no remote copies, remote signals or barrier semaphores. Data moves between devices by JAX's collectives and lax.ppermute only.
A program may use at most 32 MiB of HBM per device.

v0:
```python
import jax
import jax.numpy as jnp
from jax import lax
from jax.sharding import Mesh
from jax.sharding import PartitionSpec as P


REP = ("rep_0", "rep_1")


def wide(x):
    return x.astype(jnp.float32)


def narrow(x):
    return x.astype(jnp.bfloat16)


def pick(x, k, dim):
    return lax.dynamic_index_in_dim(x, k, dim, keepdims=False)


def turn(x, axis, step):
    n = lax.axis_size(axis)
    return lax.ppermute(x, axis, [(k, (k + step) % n) for k in range(n)])


def block(own, k, h):
    n, _, rows, columns = own.shape
    half = rows // 2
    return lax.dynamic_slice(own, (0, k, h * half, 0), (n, 1, half, columns))[:, 0]


def tagged(x, step):
    return turn(x, "rep_1", step)


def x_sum(own, m):
    up, across, down = ((m + s) % 4 for s in (1, 2, 3))
    ends = block(own, across, 0), block(own, across, 1)
    own, *ends = lax.optimization_barrier((own, *ends))
    onward = tagged(ends[0], 1)
    back = tagged(ends[1], 3)
    from_down = tagged(block(own, up, 1), 1)
    from_up = tagged(block(own, down, 0), 3)
    onward, back = lax.optimization_barrier((onward, back))
    onward = tagged(narrow(wide(block(own, up, 0)) + wide(onward)), 1)
    back = tagged(narrow(wide(block(own, down, 1)) + wide(back)), 3)
    parts = (from_down, from_up, onward, back)
    from_down, from_up, onward, back = lax.optimization_barrier(parts)
    first = wide(block(own, m, 0)) + wide(from_up) + wide(onward)
    second = wide(block(own, m, 1)) + wide(from_down) + wide(back)
    return jnp.concatenate((first, second), axis=1)


def x_gather(rows, m):
    pods, n, depth, columns = rows.shape
    half = pods // 2
    first, second = (
        part.swapaxes(0, 1).reshape(n, half * depth, columns)
        for part in (rows[:half], rows[half:])
    )
    up, across, down = ((m + s) % 4 for s in (1, 2, 3))
    down_first = tagged(first, 1)
    up_second = tagged(second, 3)
    down_second = tagged(second, 1)
    up_first = tagged(first, 3)
    across_first = tagged(down_first, 1)
    across_second = tagged(up_second, 3)
    out = jnp.zeros((n, 4, pods * depth, columns), rows.dtype)
    pieces = (
        (first, m, 0),
        (second, m, half * depth),
        (down_first, down, 0),
        (up_second, up, half * depth),
        (down_second, down, half * depth),
        (up_first, up, 0),
        (across_first, across, 0),
        (across_second, across, half * depth),
    )
    for piece, k, row in pieces:
        out = lax.dynamic_update_slice(out, piece[:, None], (0, k, row, 0))
    return out, across_first


def z_all(x, q):
    n = lax.axis_size("rep_0")
    seen = jnp.stack([x, *(turn(x, "rep_0", s) for s in range(1, n))])
    return [pick(seen, (q - k) % n, 0) for k in range(n)]


def step(deltas, pod_momentum, global_momentum, master):
    m, q = lax.axis_index("rep_1"), lax.axis_index("rep_0")
    pods = lax.axis_size("outer")
    n0 = lax.axis_size("rep_0")
    replicas = n0 * lax.axis_size("rep_1")
    columns = deltas.shape[-1]
    own = deltas[0, 0].reshape(n0, 4, -1, columns)
    rest = jnp.stack(z_all(master[0] - 0.448 * global_momentum[0], q))
    total = x_sum(own, m)
    mine = jnp.arange(n0)[:, None, None] == q
    update = (1.9 / replicas) * total + jnp.where(mine, 0.81 * pod_momentum, 0.0)
    blocks = narrow(update).reshape(n0, pods, -1, columns).swapaxes(0, 1)
    blocks = lax.all_to_all(blocks, "outer", 0, 0, tiled=True)
    by_z = z_all(narrow(jnp.sum(wide(blocks), axis=0)), q)
    glob_mean = sum(wide(part) for part in by_z) / pods
    fresh = narrow(rest - 1.26 * glob_mean)
    glob_new = 0.8 * global_momentum[0] + pick(glob_mean, q, 0)
    sent = [narrow(pick(total, (q + s) % n0, 0)) for s in (1, 2)]
    kept = pick(total, q, 0)
    fresh, sent, kept = lax.optimization_barrier((fresh, sent, kept))
    copies = jnp.broadcast_to(fresh[None], (pods, *fresh.shape))
    rows = lax.all_to_all(copies, "outer", 0, 0, tiled=True)
    others = [turn(part, "rep_0", s) for part, s in zip(sent, (1, 2), strict=True)]
    out, late = x_gather(rows, m)
    others, _ = lax.optimization_barrier((others, late))
    pod_total = kept + sum(wide(part) for part in others)
    pod_new = 0.9 * pod_momentum[0] + pod_total / replicas
    return (out.reshape(-1, columns), pod_new[None], glob_new[None])


def solution(mesh):
    finer = Mesh(
        mesh.devices.reshape(mesh.shape["outer"], 3, 4, mesh.shape["mp"]),
        ("outer", "rep_0", "rep_1", "mp"),
    )
    return jax.shard_map(
        step,
        mesh=finer,
        in_specs=(
            P("outer", REP, None, "mp"),
            P("outer", REP, "mp"),
            P(REP, "outer", "mp"),
            P(REP, "outer", "mp"),
        ),
        out_specs=(P(None, "mp"), P("outer", REP, "mp"), P(REP, "outer", "mp")),
        check_vma=False,
    )
```

profile of v0, /device:TPU:198, one launch (start us, length us, event | category | flops | bytes accessed | tf_op | source)
XLA Modules:
  0.0 144.0 jit_solution(4495142636337440744)
XLA Ops:
  0.6 0.0 copy-start.1
  0.7 1.2 dynamic-slice_bitcast_fusion.2
  1.8 2.4 %collective-permute-start.4 = (bf16[3,32,1792]{2,1,0:T(8,128)(2,1)S(1)}, bf16[3,32,1792]{2,1,0:T(8,128)(2,1)S(1)}, u32[]{:S(2)}, u32[]{:S(2)}) collective-permute-start(bf16[3,32,1792]{2,1,0:T(8,128)(2,1)S(1)} %get-tuple-element.19), channel_id=1, source_target_pairs={{0,8},{8,16},{16,24},{24,0},{1,9},{9,17},{17,25},{25,1},{2,10},{10... | collective-permute-start | bytes 1032200 | tf_op jit(solution)/shard_map/ppermute | solution.py:25
  4.2 3.5 %collective-permute-start.5 = (bf16[3,32,1792]{2,1,0:T(8,128)(2,1)S(1)}, bf16[3,32,1792]{2,1,0:T(8,128)(2,1)S(1)}, u32[]{:S(2)}, u32[]{:S(2)}) collective-permute-start(bf16[3,32,1792]{2,1,0:T(8,128)(2,1)S(1)} %get-tuple-element.20), channel_id=1, source_target_pairs={{0,24},{8,0},{16,8},{24,16},{1,25},{9,1},{17,9},{25,17},{2,26},{10... | collective-permute-start | bytes 1032200 | tf_op jit(solution)/shard_map/ppermute | solution.py:25
  7.7 1.1 dynamic-slice_bitcast_fusion
  8.9 3.6 %collective-permute-start.2 = (bf16[3,32,1792]{2,1,0:T(8,128)(2,1)S(1)}, bf16[3,32,1792]{2,1,0:T(8,128)(2,1)S(1)}, u32[]{:S(2)}, u32[]{:S(2)}) collective-permute-start(bf16[3,32,1792]{2,1,0:T(8,128)(2,1)S(1)} %get-tuple-element.38), channel_id=1, source_target_pairs={{0,8},{8,16},{16,24},{24,0},{1,9},{9,17},{17,25},{25,1},{2,10},{10... | collective-permute-start | bytes 1032200 | tf_op jit(solution)/shard_map/ppermute | solution.py:25
  12.5 2.2 %collective-permute-start.3 = (bf16[3,32,1792]{2,1,0:T(8,128)(2,1)S(1)}, bf16[3,32,1792]{2,1,0:T(8,128)(2,1)}, u32[]{:S(2)}, u32[]{:S(2)}) collective-permute-start(bf16[3,32,1792]{2,1,0:T(8,128)(2,1)S(1)} %get-tuple-element.37), channel_id=1, source_target_pairs={{0,24},{8,0},{16,8},{24,16},{1,25},{9,1},{17,9},{25,17},{2,26},{10... | collective-permute-start | bytes 1032200 | tf_op jit(solution)/shard_map/ppermute | solution.py:25
  14.8 0.0 collective-permute-done.4
  14.8 2.1 %collective-permute-done.5 = bf16[3,32,1792]{2,1,0:T(8,128)(2,1)S(1)} collective-permute-done((bf16[3,32,1792]{2,1,0:T(8,128)(2,1)S(1)}, bf16[3,32,1792]{2,1,0:T(8,128)(2,1)S(1)}, u32[]{:S(2)}, u32[]{:S(2)}) %collective-permute-start.5) | collective-permute-done | bytes 344096 | tf_op jit(solution)/shard_map/ppermute | solution.py:25
  16.9 1.2 fusion.5
  18.1 3.1 %collective-permute-start.6 = (bf16[3,32,1792]{2,1,0:T(8,128)(2,1)S(1)}, bf16[3,32,1792]{2,1,0:T(8,128)(2,1)S(1)}, u32[]{:S(2)}, u32[]{:S(2)}) collective-permute-start(bf16[3,32,1792]{2,1,0:T(8,128)(2,1)S(1)} %get-tuple-element.36), channel_id=1, source_target_pairs={{0,8},{8,16},{16,24},{24,0},{1,9},{9,17},{17,25},{25,1},{2,10},{10... | collective-permute-start | bytes 1032200 | tf_op jit(solution)/shard_map/ppermute | solution.py:25
  21.2 2.8 %collective-permute-start.7 = (bf16[3,32,1792]{2,1,0:T(8,128)(2,1)S(1)}, bf16[3,32,1792]{2,1,0:T(8,128)(2,1)S(1)}, u32[]{:S(2)}, u32[]{:S(2)}) collective-permute-start(bf16[3,32,1792]{2,1,0:T(8,128)(2,1)S(1)} %get-tuple-element.35), channel_id=1, source_target_pairs={{0,24},{8,0},{16,8},{24,16},{1,25},{9,1},{17,9},{25,17},{2,26},{10... | collective-permute-start | bytes 1032200 | tf_op jit(solution)/shard_map/ppermute | solution.py:25
  24.0 0.0 copy-done.1
  24.0 0.0 collective-permute-done.2
  24.0 0.6 collective-permute-done.3
  24.7 4.0 %collective-permute-done.6 = bf16[3,32,1792]{2,1,0:T(8,128)(2,1)S(1)} collective-permute-done((bf16[3,32,1792]{2,1,0:T(8,128)(2,1)S(1)}, bf16[3,32,1792]{2,1,0:T(8,128)(2,1)S(1)}, u32[]{:S(2)}, u32[]{:S(2)}) %collective-permute-start.6) | collective-permute-done | bytes 344096 | tf_op jit(solution)/shard_map/ppermute | solution.py:25
  28.7 3.7 %collective-permute-done.7 = bf16[3,32,1792]{2,1,0:T(8,128)(2,1)S(1)} collective-permute-done((bf16[3,32,1792]{2,1,0:T(8,128)(2,1)S(1)}, bf16[3,32,1792]{2,1,0:T(8,128)(2,1)S(1)}, u32[]{:S(2)}, u32[]{:S(2)}) %collective-permute-start.7) | collective-permute-done | bytes 344096 | tf_op jit(solution)/shard_map/ppermute | solution.py:25
  32.4 1.4 fusion.4
  33.8 0.0 copy-start.2
  33.8 0.0 copy-start.3
  33.8 1.1 fusion.3
  34.9 7.1 %all-to-all-start = ((bf16[8,3,8,1792]{3,2,1,0:T(8,128)(2,1)}), bf16[8,3,8,1792]{3,2,1,0:T(8,128)(2,1)S(1)}, u32[]{:S(2)}, u32[]{:S(2)}) async-start(bf16[8,3,8,1792]{3,2,1,0:T(8,128)(2,1)} %fusion.3), calls=%async_computation | async-start | bytes 1376256 | tf_op jit(solution)/shard_map/all_to_all | solution.py:104
  42.0 0.0 copy-done.2
  42.0 0.0 copy-done.3
  42.0 10.6 %collective-permute-start = (f32[8,1792]{1,0:T(8,128)S(1)}, f32[8,1792]{1,0:T(8,128)S(1)}, u32[]{:S(2)}, u32[]{:S(2)}) collective-permute-start(f32[8,1792]{1,0:T(8,128)S(1)} %bitcast.107), channel_id=1, source_target_pairs={{0,32},{32,64},{64,0},{1,33},{33,65},{65,1},{2,34},{34,66},{66,2},... | collective-permute-start | bytes 172040 | tf_op jit(solution)/shard_map/ppermute | solution.py:25
  52.7 3.2 %collective-permute-start.1 = (f32[8,1792]{1,0:T(8,128)S(1)}, f32[8,1792]{1,0:T(8,128)S(1)}, u32[]{:S(2)}, u32[]{:S(2)}) collective-permute-start(f32[8,1792]{1,0:T(8,128)S(1)} %bitcast.108), channel_id=1, source_target_pairs={{0,64},{32,0},{64,32},{1,65},{33,1},{65,33},{2,66},{34,2},{66,34},... | collective-permute-start | bytes 172040 | tf_op jit(solution)/shard_map/ppermute | solution.py:25
  55.9 1.9 %collective-permute-done = f32[8,1792]{1,0:T(8,128)S(1)} collective-permute-done((f32[8,1792]{1,0:T(8,128)S(1)}, f32[8,1792]{1,0:T(8,128)S(1)}, u32[]{:S(2)}, u32[]{:S(2)}) %collective-permute-start) | collective-permute-done | bytes 57376 | tf_op jit(solution)/shard_map/ppermute | solution.py:25
  57.8 4.8 %collective-permute-done.1 = f32[8,1792]{1,0:T(8,128)S(1)} collective-permute-done((f32[8,1792]{1,0:T(8,128)S(1)}, f32[8,1792]{1,0:T(8,128)S(1)}, u32[]{:S(2)}, u32[]{:S(2)}) %collective-permute-start.1) | collective-permute-done | bytes 57376 | tf_op jit(solution)/shard_map/ppermute | solution.py:25
  62.7 0.0 all-to-all-done
  62.7 0.1 reduce_sum.12
  62.8 8.3 %collective-permute-start.8 = (bf16[3,8,1792]{2,1,0:T(8,128)(2,1)S(1)}, bf16[3,8,1792]{2,1,0:T(8,128)(2,1)S(1)}, u32[]{:S(2)}, u32[]{:S(2)}) collective-permute-start(bf16[3,8,1792]{2,1,0:T(8,128)(2,1)S(1)} %reduce_sum.12), channel_id=1, source_target_pairs={{0,32},{32,64},{64,0},{1,33},{33,65},{65,1},{2,34},{34,66},{66,2},... | collective-permute-start | bytes 258056 | tf_op jit(solution)/shard_map/ppermute | solution.py:25
  71.2 3.2 %collective-permute-start.9 = (bf16[3,8,1792]{2,1,0:T(8,128)(2,1)S(1)}, bf16[3,8,1792]{2,1,0:T(8,128)(2,1)S(1)}, u32[]{:S(2)}, u32[]{:S(2)}) collective-permute-start(bf16[3,8,1792]{2,1,0:T(8,128)(2,1)S(1)} %reduce_sum.12), channel_id=1, source_target_pairs={{0,64},{32,0},{64,32},{1,65},{33,1},{65,33},{2,66},{34,2},{66,34},... | collective-permute-start | bytes 258056 | tf_op jit(solution)/shard_map/ppermute | solution.py:25
  74.3 0.1 fusion.15
  74.4 3.2 %collective-permute-done.8 = bf16[3,8,1792]{2,1,0:T(8,128)(2,1)S(1)} collective-permute-done((bf16[3,8,1792]{2,1,0:T(8,128)(2,1)S(1)}, bf16[3,8,1792]{2,1,0:T(8,128)(2,1)S(1)}, u32[]{:S(2)}, u32[]{:S(2)}) %collective-permute-start.8) | collective-permute-done | bytes 86048 | tf_op jit(solution)/shard_map/ppermute | solution.py:25
  77.6 3.9 %collective-permute-done.9 = bf16[3,8,1792]{2,1,0:T(8,128)(2,1)S(1)} collective-permute-done((bf16[3,8,1792]{2,1,0:T(8,128)(2,1)S(1)}, bf16[3,8,1792]{2,1,0:T(8,128)(2,1)S(1)}, u32[]{:S(2)}, u32[]{:S(2)}) %collective-permute-start.9) | collective-permute-done | bytes 86048 | tf_op jit(solution)/shard_map/ppermute | solution.py:25
  81.5 0.1 fusion.17
  81.6 0.9 broadcast_in_dim.59
  82.5 5.3 %all-to-all-start.1 = ((bf16[8,3,8,1792]{3,2,1,0:T(8,128)(2,1)}), bf16[8,3,8,1792]{3,2,1,0:T(8,128)(2,1)S(1)}, u32[]{:S(2)}, u32[]{:S(2)}) async-start(bf16[8,3,8,1792]{3,2,1,0:T(8,128)(2,1)} %broadcast_in_dim.59), calls=%async_computation.1 | async-start | bytes 1376256 | tf_op jit(solution)/shard_map/all_to_all | solution.py:113
  87.7 5.2 %collective-permute-start.16 = (bf16[64,1792]{1,0:T(8,128)(2,1)S(1)}, bf16[64,1792]{1,0:T(8,128)(2,1)S(1)}, u32[]{:S(2)}, u32[]{:S(2)}) collective-permute-start(bf16[64,1792]{1,0:T(8,128)(2,1)S(1)} %get-tuple-element.29), channel_id=1, source_target_pairs={{0,32},{32,64},{64,0},{1,33},{33,65},{65,1},{2,34},{34,66},{66,2},... | collective-permute-start | bytes 688136 | tf_op jit(solution)/shard_map/ppermute | solution.py:25
  93.0 4.5 %collective-permute-start.17 = (bf16[64,1792]{1,0:T(8,128)(2,1)S(1)}, bf16[64,1792]{1,0:T(8,128)(2,1)S(1)}, u32[]{:S(2)}, u32[]{:S(2)}) collective-permute-start(bf16[64,1792]{1,0:T(8,128)(2,1)S(1)} %get-tuple-element.30), channel_id=1, source_target_pairs={{0,64},{32,0},{64,32},{1,65},{33,1},{65,33},{2,66},{34,2},{66,34},... | collective-permute-start | bytes 688136 | tf_op jit(solution)/shard_map/ppermute | solution.py:25
  97.5 0.6 fusion.19
  98.1 5.8 %all-to-all-done.1 = bf16[8,3,8,1792]{3,2,1,0:T(8,128)(2,1)S(1)} async-done(((bf16[8,3,8,1792]{3,2,1,0:T(8,128)(2,1)}), bf16[8,3,8,1792]{3,2,1,0:T(8,128)(2,1)S(1)}, u32[]{:S(2)}, u32[]{:S(2)}) %all-to-all-start.1) | async-done | bytes 688160 | tf_op jit(solution)/shard_map/all_to_all | solution.py:113
  104.0 4.4 %collective-permute-start.11 = (bf16[3,32,1792]{2,1,0:T(8,128)(2,1)S(1)}, bf16[3,32,1792]{2,1,0:T(8,128)(2,1)S(1)}, u32[]{:S(2)}, u32[]{:S(2)}) collective-permute-start(bf16[3,32,1792]{2,1,0:T(8,128)(2,1)S(1)} %bitcast.104), channel_id=1, source_target_pairs={{0,24},{8,0},{16,8},{24,16},{1,25},{9,1},{17,9},{25,17},{2,26},{10... | collective-permute-start | bytes 1032200 | tf_op jit(solution)/shard_map/ppermute | solution.py:25
  108.4 2.6 %collective-permute-start.12 = (bf16[3,32,1792]{2,1,0:T(8,128)(2,1)S(1)}, bf16[3,32,1792]{2,1,0:T(8,128)(2,1)S(1)}, u32[]{:S(2)}, u32[]{:S(2)}) collective-permute-start(bf16[3,32,1792]{2,1,0:T(8,128)(2,1)S(1)} %bitcast.105), channel_id=1, source_target_pairs={{0,8},{8,16},{16,24},{24,0},{1,9},{9,17},{17,25},{25,1},{2,10},{10... | collective-permute-start | bytes 1032200 | tf_op jit(solution)/shard_map/ppermute | solution.py:25
  111.1 1.9 %collective-permute-start.10 = (bf16[3,32,1792]{2,1,0:T(8,128)(2,1)S(1)}, bf16[3,32,1792]{2,1,0:T(8,128)(2,1)S(1)}, u32[]{:S(2)}, u32[]{:S(2)}) collective-permute-start(bf16[3,32,1792]{2,1,0:T(8,128)(2,1)S(1)} %bitcast.102), channel_id=1, source_target_pairs={{0,8},{8,16},{16,24},{24,0},{1,9},{9,17},{17,25},{25,1},{2,10},{10... | collective-permute-start | bytes 1032200 | tf_op jit(solution)/shard_map/ppermute | solution.py:25
  113.0 0.2 broadcast_in_dim.54
  113.3 11.4 %collective-permute-done.10 = bf16[3,32,1792]{2,1,0:T(8,128)(2,1)S(1)} collective-permute-done((bf16[3,32,1792]{2,1,0:T(8,128)(2,1)S(1)}, bf16[3,32,1792]{2,1,0:T(8,128)(2,1)S(1)}, u32[]{:S(2)}, u32[]{:S(2)}) %collective-permute-start.10) | collective-permute-done | bytes 344096 | tf_op jit(solution)/shard_map/ppermute | solution.py:25
  124.7 2.2 %collective-permute-start.13 = (bf16[3,32,1792]{2,1,0:T(8,128)(2,1)S(1)}, bf16[3,32,1792]{2,1,0:T(8,128)(2,1)S(1)}, u32[]{:S(2)}, u32[]{:S(2)}) collective-permute-start(bf16[3,32,1792]{2,1,0:T(8,128)(2,1)S(1)} %bitcast.103), channel_id=1, source_target_pairs={{0,24},{8,0},{16,8},{24,16},{1,25},{9,1},{17,9},{25,17},{2,26},{10... | collective-permute-start | bytes 1032200 | tf_op jit(solution)/shard_map/ppermute | solution.py:25
  127.0 0.0 collective-permute-done.11
  127.0 4.9 %collective-permute-start.14 = (bf16[3,32,1792]{2,1,0:T(8,128)(2,1)S(1)}, bf16[3,32,1792]{2,1,0:T(8,128)(2,1)S(1)}, u32[]{:S(2)}, u32[]{:S(2)}) collective-permute-start(bf16[3,32,1792]{2,1,0:T(8,128)(2,1)S(1)} %collective-permute-done.10), channel_id=1, source_target_pairs={{0,8},{8,16},{16,24},{24,0},{1,9},{9,17},{17,25},{25,1},{2,10},{10... | collective-permute-start | bytes 1032200 | tf_op jit(solution)/shard_map/ppermute | solution.py:25
  131.9 0.0 collective-permute-done.12
  131.9 1.9 %collective-permute-start.15 = (bf16[3,32,1792]{2,1,0:T(8,128)(2,1)S(1)}, bf16[3,32,1792]{2,1,0:T(8,128)(2,1)S(1)}, u32[]{:S(2)}, u32[]{:S(2)}) collective-permute-start(bf16[3,32,1792]{2,1,0:T(8,128)(2,1)S(1)} %collective-permute-done.11), channel_id=1, source_target_pairs={{0,24},{8,0},{16,8},{24,16},{1,25},{9,1},{17,9},{25,17},{2,26},{10... | collective-permute-start | bytes 1032200 | tf_op jit(solution)/shard_map/ppermute | solution.py:25
  133.9 3.0 %collective-permute-done.13 = bf16[3,32,1792]{2,1,0:T(8,128)(2,1)S(1)} collective-permute-done((bf16[3,32,1792]{2,1,0:T(8,128)(2,1)S(1)}, bf16[3,32,1792]{2,1,0:T(8,128)(2,1)S(1)}, u32[]{:S(2)}, u32[]{:S(2)}) %collective-permute-start.13) | collective-permute-done | bytes 344096 | tf_op jit(solution)/shard_map/ppermute | solution.py:25
  136.9 0.0 collective-permute-done.16
  136.9 0.0 collective-permute-done.17
  136.9 0.0 collective-permute-done.14
  136.9 0.9 fusion.14
  137.8 4.6 %collective-permute-done.15 = bf16[3,32,1792]{2,1,0:T(8,128)(2,1)S(1)} collective-permute-done((bf16[3,32,1792]{2,1,0:T(8,128)(2,1)S(1)}, bf16[3,32,1792]{2,1,0:T(8,128)(2,1)S(1)}, u32[]{:S(2)}, u32[]{:S(2)}) %collective-permute-start.15) | collective-permute-done | bytes 344096 | tf_op jit(solution)/shard_map/ppermute | solution.py:25
  142.5 0.0 copy-start
  142.5 1.5 %copy-done = bf16[3,4,64,1792]{3,2,1,0:T(8,128)(2,1)} copy-done((bf16[3,4,64,1792]{3,2,1,0:T(8,128)(2,1)}, bf16[3,4,64,1792]{3,2,1,0:T(8,128)(2,1)S(1)}, u32[]{:S(2)}) %copy-start) | copy-done | bytes 2752536
  (18 shorter events, 0.5 us)
Async XLA Ops:
  0.6 23.3 %copy-start.1 = (f32[1,64,1792]{2,1,0:T(8,128)S(1)}, f32[1,64,1792]{2,1,0:T(8,128)}, u32[]{:S(2)}) copy-start(f32[1,64,1792]{2,1,0:T(8,128)} %param.5) | copy-start | bytes 1376260
  1.8 12.9 %collective-permute-start.4 = (bf16[3,32,1792]{2,1,0:T(8,128)(2,1)S(1)}, bf16[3,32,1792]{2,1,0:T(8,128)(2,1)S(1)}, u32[]{:S(2)}, u32[]{:S(2)}) collective-permute-start(bf16[3,32,1792]{2,1,0:T(8,128)(2,1)S(1)} %get-tuple-element.19), channel_id=1, source_target_pairs={{0,8},{8,16},{16,24},{24,0},{1,9},{9,17},{17,25},{25,1},{2,10},{10... | collective-permute-start | bytes 1032200 | tf_op jit(solution)/shard_map/ppermute | solution.py:25
  4.2 12.6 %collective-permute-start.5 = (bf16[3,32,1792]{2,1,0:T(8,128)(2,1)S(1)}, bf16[3,32,1792]{2,1,0:T(8,128)(2,1)S(1)}, u32[]{:S(2)}, u32[]{:S(2)}) collective-permute-start(bf16[3,32,1792]{2,1,0:T(8,128)(2,1)S(1)} %get-tuple-element.20), channel_id=1, source_target_pairs={{0,24},{8,0},{16,8},{24,16},{1,25},{9,1},{17,9},{25,17},{2,26},{10... | collective-permute-start | bytes 1032200 | tf_op jit(solution)/shard_map/ppermute | solution.py:25
  8.9 15.2 %collective-permute-start.2 = (bf16[3,32,1792]{2,1,0:T(8,128)(2,1)S(1)}, bf16[3,32,1792]{2,1,0:T(8,128)(2,1)S(1)}, u32[]{:S(2)}, u32[]{:S(2)}) collective-permute-start(bf16[3,32,1792]{2,1,0:T(8,128)(2,1)S(1)} %get-tuple-element.38), channel_id=1, source_target_pairs={{0,8},{8,16},{16,24},{24,0},{1,9},{9,17},{17,25},{25,1},{2,10},{10... | collective-permute-start | bytes 1032200 | tf_op jit(solution)/shard_map/ppermute | solution.py:25
  12.5 12.2 %collective-permute-start.3 = (bf16[3,32,1792]{2,1,0:T(8,128)(2,1)S(1)}, bf16[3,32,1792]{2,1,0:T(8,128)(2,1)}, u32[]{:S(2)}, u32[]{:S(2)}) collective-permute-start(bf16[3,32,1792]{2,1,0:T(8,128)(2,1)S(1)} %get-tuple-element.37), channel_id=1, source_target_pairs={{0,24},{8,0},{16,8},{24,16},{1,25},{9,1},{17,9},{25,17},{2,26},{10... | collective-permute-start | bytes 1032200 | tf_op jit(solution)/shard_map/ppermute | solution.py:25
  18.1 10.6 %collective-permute-start.6 = (bf16[3,32,1792]{2,1,0:T(8,128)(2,1)S(1)}, bf16[3,32,1792]{2,1,0:T(8,128)(2,1)S(1)}, u32[]{:S(2)}, u32[]{:S(2)}) collective-permute-start(bf16[3,32,1792]{2,1,0:T(8,128)(2,1)S(1)} %get-tuple-element.36), channel_id=1, source_target_pairs={{0,8},{8,16},{16,24},{24,0},{1,9},{9,17},{17,25},{25,1},{2,10},{10... | collective-permute-start | bytes 1032200 | tf_op jit(solution)/shard_map/ppermute | solution.py:25
  21.2 11.2 %collective-permute-start.7 = (bf16[3,32,1792]{2,1,0:T(8,128)(2,1)S(1)}, bf16[3,32,1792]{2,1,0:T(8,128)(2,1)S(1)}, u32[]{:S(2)}, u32[]{:S(2)}) collective-permute-start(bf16[3,32,1792]{2,1,0:T(8,128)(2,1)S(1)} %get-tuple-element.35), channel_id=1, source_target_pairs={{0,24},{8,0},{16,8},{24,16},{1,25},{9,1},{17,9},{25,17},{2,26},{10... | collective-permute-start | bytes 1032200 | tf_op jit(solution)/shard_map/ppermute | solution.py:25
  33.8 8.2 %copy-start.2 = (f32[1,8,1792]{2,1,0:T(8,128)S(1)}, f32[1,8,1792]{2,1,0:T(8,128)}, u32[]{:S(2)}) copy-start(f32[1,8,1792]{2,1,0:T(8,128)} %param.6) | copy-start | bytes 172036
  33.8 8.2 %copy-start.3 = (f32[1,8,1792]{2,1,0:T(8,128)S(1)}, f32[1,8,1792]{2,1,0:T(8,128)}, u32[]{:S(2)}) copy-start(f32[1,8,1792]{2,1,0:T(8,128)} %param.7) | copy-start | bytes 172036
  34.9 27.8 %all-to-all-start = ((bf16[8,3,8,1792]{3,2,1,0:T(8,128)(2,1)}), bf16[8,3,8,1792]{3,2,1,0:T(8,128)(2,1)S(1)}, u32[]{:S(2)}, u32[]{:S(2)}) async-start(bf16[8,3,8,1792]{3,2,1,0:T(8,128)(2,1)} %fusion.3), calls=%async_computation | async-start | bytes 1376256 | tf_op jit(solution)/shard_map/all_to_all | solution.py:104
  42.0 15.8 %collective-permute-start = (f32[8,1792]{1,0:T(8,128)S(1)}, f32[8,1792]{1,0:T(8,128)S(1)}, u32[]{:S(2)}, u32[]{:S(2)}) collective-permute-start(f32[8,1792]{1,0:T(8,128)S(1)} %bitcast.107), channel_id=1, source_target_pairs={{0,32},{32,64},{64,0},{1,33},{33,65},{65,1},{2,34},{34,66},{66,2},... | collective-permute-start | bytes 172040 | tf_op jit(solution)/shard_map/ppermute | solution.py:25
  52.7 10.0 %collective-permute-start.1 = (f32[8,1792]{1,0:T(8,128)S(1)}, f32[8,1792]{1,0:T(8,128)S(1)}, u32[]{:S(2)}, u32[]{:S(2)}) collective-permute-start(f32[8,1792]{1,0:T(8,128)S(1)} %bitcast.108), channel_id=1, source_target_pairs={{0,64},{32,0},{64,32},{1,65},{33,1},{65,33},{2,66},{34,2},{66,34},... | collective-permute-start | bytes 172040 | tf_op jit(solution)/shard_map/ppermute | solution.py:25
  62.8 14.7 %collective-permute-start.8 = (bf16[3,8,1792]{2,1,0:T(8,128)(2,1)S(1)}, bf16[3,8,1792]{2,1,0:T(8,128)(2,1)S(1)}, u32[]{:S(2)}, u32[]{:S(2)}) collective-permute-start(bf16[3,8,1792]{2,1,0:T(8,128)(2,1)S(1)} %reduce_sum.12), channel_id=1, source_target_pairs={{0,32},{32,64},{64,0},{1,33},{33,65},{65,1},{2,34},{34,66},{66,2},... | collective-permute-start | bytes 258056 | tf_op jit(solution)/shard_map/ppermute | solution.py:25
  71.2 10.3 %collective-permute-start.9 = (bf16[3,8,1792]{2,1,0:T(8,128)(2,1)S(1)}, bf16[3,8,1792]{2,1,0:T(8,128)(2,1)S(1)}, u32[]{:S(2)}, u32[]{:S(2)}) collective-permute-start(bf16[3,8,1792]{2,1,0:T(8,128)(2,1)S(1)} %reduce_sum.12), channel_id=1, source_target_pairs={{0,64},{32,0},{64,32},{1,65},{33,1},{65,33},{2,66},{34,2},{66,34},... | collective-permute-start | bytes 258056 | tf_op jit(solution)/shard_map/ppermute | solution.py:25
  82.5 21.4 %all-to-all-start.1 = ((bf16[8,3,8,1792]{3,2,1,0:T(8,128)(2,1)}), bf16[8,3,8,1792]{3,2,1,0:T(8,128)(2,1)S(1)}, u32[]{:S(2)}, u32[]{:S(2)}) async-start(bf16[8,3,8,1792]{3,2,1,0:T(8,128)(2,1)} %broadcast_in_dim.59), calls=%async_computation.1 | async-start | bytes 1376256 | tf_op jit(solution)/shard_map/all_to_all | solution.py:113
  87.7 49.2 %collective-permute-start.16 = (bf16[64,1792]{1,0:T(8,128)(2,1)S(1)}, bf16[64,1792]{1,0:T(8,128)(2,1)S(1)}, u32[]{:S(2)}, u32[]{:S(2)}) collective-permute-start(bf16[64,1792]{1,0:T(8,128)(2,1)S(1)} %get-tuple-element.29), channel_id=1, source_target_pairs={{0,32},{32,64},{64,0},{1,33},{33,65},{65,1},{2,34},{34,66},{66,2},... | collective-permute-start | bytes 688136 | tf_op jit(solution)/shard_map/ppermute | solution.py:25
  93.0 44.0 %collective-permute-start.17 = (bf16[64,1792]{1,0:T(8,128)(2,1)S(1)}, bf16[64,1792]{1,0:T(8,128)(2,1)S(1)}, u32[]{:S(2)}, u32[]{:S(2)}) collective-permute-start(bf16[64,1792]{1,0:T(8,128)(2,1)S(1)} %get-tuple-element.30), channel_id=1, source_target_pairs={{0,64},{32,0},{64,32},{1,65},{33,1},{65,33},{2,66},{34,2},{66,34},... | collective-permute-start | bytes 688136 | tf_op jit(solution)/shard_map/ppermute | solution.py:25
  104.0 23.0 %collective-permute-start.11 = (bf16[3,32,1792]{2,1,0:T(8,128)(2,1)S(1)}, bf16[3,32,1792]{2,1,0:T(8,128)(2,1)S(1)}, u32[]{:S(2)}, u32[]{:S(2)}) collective-permute-start(bf16[3,32,1792]{2,1,0:T(8,128)(2,1)S(1)} %bitcast.104), channel_id=1, source_target_pairs={{0,24},{8,0},{16,8},{24,16},{1,25},{9,1},{17,9},{25,17},{2,26},{10... | collective-permute-start | bytes 1032200 | tf_op jit(solution)/shard_map/ppermute | solution.py:25
  108.4 23.5 %collective-permute-start.12 = (bf16[3,32,1792]{2,1,0:T(8,128)(2,1)S(1)}, bf16[3,32,1792]{2,1,0:T(8,128)(2,1)S(1)}, u32[]{:S(2)}, u32[]{:S(2)}) collective-permute-start(bf16[3,32,1792]{2,1,0:T(8,128)(2,1)S(1)} %bitcast.105), channel_id=1, source_target_pairs={{0,8},{8,16},{16,24},{24,0},{1,9},{9,17},{17,25},{25,1},{2,10},{10... | collective-permute-start | bytes 1032200 | tf_op jit(solution)/shard_map/ppermute | solution.py:25
  111.1 13.7 %collective-permute-start.10 = (bf16[3,32,1792]{2,1,0:T(8,128)(2,1)S(1)}, bf16[3,32,1792]{2,1,0:T(8,128)(2,1)S(1)}, u32[]{:S(2)}, u32[]{:S(2)}) collective-permute-start(bf16[3,32,1792]{2,1,0:T(8,128)(2,1)S(1)} %bitcast.102), channel_id=1, source_target_pairs={{0,8},{8,16},{16,24},{24,0},{1,9},{9,17},{17,25},{25,1},{2,10},{10... | collective-permute-start | bytes 1032200 | tf_op jit(solution)/shard_map/ppermute | solution.py:25
  124.7 12.1 %collective-permute-start.13 = (bf16[3,32,1792]{2,1,0:T(8,128)(2,1)S(1)}, bf16[3,32,1792]{2,1,0:T(8,128)(2,1)S(1)}, u32[]{:S(2)}, u32[]{:S(2)}) collective-permute-start(bf16[3,32,1792]{2,1,0:T(8,128)(2,1)S(1)} %bitcast.103), channel_id=1, source_target_pairs={{0,24},{8,0},{16,8},{24,16},{1,25},{9,1},{17,9},{25,17},{2,26},{10... | collective-permute-start | bytes 1032200 | tf_op jit(solution)/shard_map/ppermute | solution.py:25
  127.0 9.9 %collective-permute-start.14 = (bf16[3,32,1792]{2,1,0:T(8,128)(2,1)S(1)}, bf16[3,32,1792]{2,1,0:T(8,128)(2,1)S(1)}, u32[]{:S(2)}, u32[]{:S(2)}) collective-permute-start(bf16[3,32,1792]{2,1,0:T(8,128)(2,1)S(1)} %collective-permute-done.10), channel_id=1, source_target_pairs={{0,8},{8,16},{16,24},{24,0},{1,9},{9,17},{17,25},{25,1},{2,10},{10... | collective-permute-start | bytes 1032200 | tf_op jit(solution)/shard_map/ppermute | solution.py:25
  131.9 10.6 %collective-permute-start.15 = (bf16[3,32,1792]{2,1,0:T(8,128)(2,1)S(1)}, bf16[3,32,1792]{2,1,0:T(8,128)(2,1)S(1)}, u32[]{:S(2)}, u32[]{:S(2)}) collective-permute-start(bf16[3,32,1792]{2,1,0:T(8,128)(2,1)S(1)} %collective-permute-done.11), channel_id=1, source_target_pairs={{0,24},{8,0},{16,8},{24,16},{1,25},{9,1},{17,9},{25,17},{2,26},{10... | collective-permute-start | bytes 1032200 | tf_op jit(solution)/shard_map/ppermute | solution.py:25
  142.5 1.5 %copy-start = (bf16[3,4,64,1792]{3,2,1,0:T(8,128)(2,1)}, bf16[3,4,64,1792]{3,2,1,0:T(8,128)(2,1)S(1)}, u32[]{:S(2)}) copy-start(bf16[3,4,64,1792]{3,2,1,0:T(8,128)(2,1)S(1)} %bitcast_dynamic-update-slice_fusion) | copy-start | bytes 8257540
where the time goes:
time: 145 us; the launch traced here: 144 us
  starting transfers between devices  82.8 us (57%)
  waiting for transfers between devices  49 us (34%)
  other arithmetic  5.63 us (4%)
  local copies, waits for them, and re-layouts  5.35 us (4%)
    ppermute x18, starting transfers between devices, turn(): return lax.ppermute(x, axis, [(k, (k + step) % n) for k in range(n)])  70.5 us
    ppermute x18, waiting for transfers between devices, turn(): return lax.ppermute(x, axis, [(k, (k + step) % n) for k in range(n)])  43.2 us
    all_to_all x1, starting transfers between devices, step(): blocks = lax.all_to_all(blocks, 'outer', 0, 0, tiled=True)  7.1 us
    all_to_all x1, waiting for transfers between devices, step(): rows = lax.all_to_all(copies, 'outer', 0, 0, tiled=True)  5.75 us
    all_to_all x1, starting transfers between devices, step(): rows = lax.all_to_all(copies, 'outer', 0, 0, tiled=True)  5.28 us
  transfers between devices with their start and end apart: 20, of which 12 were waited for; matrix products, arithmetic and copies ran while one was open for 3% of the time, Pallas kernels for 0%

commit v1 on v0

--- a/solution.py
+++ b/solution.py
@@ -20,9 +20,23 @@
     return lax.dynamic_index_in_dim(x, k, dim, keepdims=False)
 
 
+def sign(core):
+    return 1 - 2 * (core % 2)
+
+
+def place(k, axis, step):
+    n = lax.axis_size(axis)
+    return (k + n + sign(lax.axis_index("mp")) * step) % n
+
+
 def turn(x, axis, step):
-    n = lax.axis_size(axis)
-    return lax.ppermute(x, axis, [(k, (k + step) % n) for k in range(n)])
+    n, width = lax.axis_size(axis), lax.axis_size("mp")
+    pairs = [
+        (k * width + c, (k + sign(c) * step) % n * width + c)
+        for k in range(n)
+        for c in range(width)
+    ]
+    return lax.ppermute(x, (axis, "mp"), pairs)
 
 
 def block(own, k, h):
@@ -36,7 +50,7 @@
 
 
 def x_sum(own, m):
-    up, across, down = ((m + s) % 4 for s in (1, 2, 3))
+    up, across, down = (place(m, "rep_1", s) for s in (1, 2, 3))
     ends = block(own, across, 0), block(own, across, 1)
     own, *ends = lax.optimization_barrier((own, *ends))
     onward = tagged(ends[0], 1)
@@ -60,7 +74,7 @@
         part.swapaxes(0, 1).reshape(n, half * depth, columns)
         for part in (rows[:half], rows[half:])
     )
-    up, across, down = ((m + s) % 4 for s in (1, 2, 3))
+    up, across, down = (place(m, "rep_1", s) for s in (1, 2, 3))
     down_first = tagged(first, 1)
     up_second = tagged(second, 3)
     down_second = tagged(second, 1)
@@ -86,7 +100,8 @@
 def z_all(x, q):
     n = lax.axis_size("rep_0")
     seen = jnp.stack([x, *(turn(x, "rep_0", s) for s in range(1, n))])
-    return [pick(seen, (q - k) % n, 0) for k in range(n)]
+    away = sign(lax.axis_index("mp"))
+    return [pick(seen, (n + away * (q - k)) % n, 0) for k in range(n)]
 
 
 def step(deltas, pod_momentum, global_momentum, master):
@@ -106,7 +121,7 @@
     glob_mean = sum(wide(part) for part in by_z) / pods
     fresh = narrow(rest - 1.26 * glob_mean)
     glob_new = 0.8 * global_momentum[0] + pick(glob_mean, q, 0)
-    sent = [narrow(pick(total, (q + s) % n0, 0)) for s in (1, 2)]
+    sent = [narrow(pick(total, place(q, "rep_0", s), 0)) for s in (1, 2)]
     kept = pick(total, q, 0)
     fresh, sent, kept = lax.optimization_barrier((fresh, sent, kept))
     copies = jnp.broadcast_to(fresh[None], (pods, *fresh.shape))

time: 145 us -> 150 us (1.034)
  the two profiles are of different devices: /device:TPU:198 before, /device:TPU:1 now
where the time goes in v1:
time: 150 us; the launch traced here: 149 us
  starting transfers between devices  85.3 us (57%)
  waiting for transfers between devices  51.9 us (35%)
  other arithmetic  5.63 us (4%)
  local copies, waits for them, and re-layouts  5.35 us (4%)
    ppermute x18, starting transfers between devices, turn(): return lax.ppermute(x, (axis, 'mp'), pairs)  74.2 us
    ppermute x18, waiting for transfers between devices, turn(): return lax.ppermute(x, (axis, 'mp'), pairs)  41.2 us
    all_to_all x1, waiting for transfers between devices, step(): rows = lax.all_to_all(copies, 'outer', 0, 0, tiled=True)  10.7 us
    all_to_all x1, starting transfers between devices, step(): blocks = lax.all_to_all(blocks, 'outer', 0, 0, tiled=True)  6.21 us
    all_to_all x1, starting transfers between devices, step(): rows = lax.all_to_all(copies, 'outer', 0, 0, tiled=True)  4.9 us
  transfers between devices with their start and end apart: 20, of which 10 were waited for; matrix products, arithmetic and copies ran while one was open for 3% of the time, Pallas kernels for 0%

profile of v1, /device:TPU:1, one launch (start us, length us, event | category | flops | bytes accessed | tf_op | source)
XLA Modules:
  0.0 149.5 jit_solution(4790500211962401082)
XLA Ops:
  0.6 0.0 copy-start.1
  0.7 1.2 dynamic-slice_bitcast_fusion.2
  1.9 5.2 %collective-permute-start.4 = (bf16[3,32,1792]{2,1,0:T(8,128)(2,1)S(1)}, bf16[3,32,1792]{2,1,0:T(8,128)(2,1)S(1)}, u32[]{:S(2)}, u32[]{:S(2)}) collective-permute-start(bf16[3,32,1792]{2,1,0:T(8,128)(2,1)S(1)} %get-tuple-element.19), channel_id=1, source_target_pairs={{0,8},{1,25},{2,10},{3,27},{4,12},{5,29},{6,14},{7,31},{8,16},{9,1... | collective-permute-start | bytes 1032200 | tf_op jit(solution)/shard_map/ppermute | solution.py:39
  7.1 1.9 %collective-permute-start.5 = (bf16[3,32,1792]{2,1,0:T(8,128)(2,1)S(1)}, bf16[3,32,1792]{2,1,0:T(8,128)(2,1)S(1)}, u32[]{:S(2)}, u32[]{:S(2)}) collective-permute-start(bf16[3,32,1792]{2,1,0:T(8,128)(2,1)S(1)} %get-tuple-element.20), channel_id=1, source_target_pairs={{0,24},{1,9},{2,26},{3,11},{4,28},{5,13},{6,30},{7,15},{8,0},{9,17... | collective-permute-start | bytes 1032200 | tf_op jit(solution)/shard_map/ppermute | solution.py:39
  9.0 1.1 dynamic-slice_bitcast_fusion
  10.2 4.6 %collective-permute-start.2 = (bf16[3,32,1792]{2,1,0:T(8,128)(2,1)S(1)}, bf16[3,32,1792]{2,1,0:T(8,128)(2,1)S(1)}, u32[]{:S(2)}, u32[]{:S(2)}) collective-permute-start(bf16[3,32,1792]{2,1,0:T(8,128)(2,1)S(1)} %get-tuple-element.38), channel_id=1, source_target_pairs={{0,8},{1,25},{2,10},{3,27},{4,12},{5,29},{6,14},{7,31},{8,16},{9,1... | collective-permute-start | bytes 1032200 | tf_op jit(solution)/shard_map/ppermute | solution.py:39
  14.8 1.9 %collective-permute-start.3 = (bf16[3,32,1792]{2,1,0:T(8,128)(2,1)S(1)}, bf16[3,32,1792]{2,1,0:T(8,128)(2,1)}, u32[]{:S(2)}, u32[]{:S(2)}) collective-permute-start(bf16[3,32,1792]{2,1,0:T(8,128)(2,1)S(1)} %get-tuple-element.37), channel_id=1, source_target_pairs={{0,24},{1,9},{2,26},{3,11},{4,28},{5,13},{6,30},{7,15},{8,0},{9,17... | collective-permute-start | bytes 1032200 | tf_op jit(solution)/shard_map/ppermute | solution.py:39
  16.7 0.0 collective-permute-done.4
  16.7 0.0 collective-permute-done.5
  16.7 1.3 fusion.5
  18.0 4.6 %collective-permute-start.6 = (bf16[3,32,1792]{2,1,0:T(8,128)(2,1)S(1)}, bf16[3,32,1792]{2,1,0:T(8,128)(2,1)S(1)}, u32[]{:S(2)}, u32[]{:S(2)}) collective-permute-start(bf16[3,32,1792]{2,1,0:T(8,128)(2,1)S(1)} %get-tuple-element.36), channel_id=1, source_target_pairs={{0,8},{1,25},{2,10},{3,27},{4,12},{5,29},{6,14},{7,31},{8,16},{9,1... | collective-permute-start | bytes 1032200 | tf_op jit(solution)/shard_map/ppermute | solution.py:39
  22.6 1.9 %collective-permute-start.7 = (bf16[3,32,1792]{2,1,0:T(8,128)(2,1)S(1)}, bf16[3,32,1792]{2,1,0:T(8,128)(2,1)S(1)}, u32[]{:S(2)}, u32[]{:S(2)}) collective-permute-start(bf16[3,32,1792]{2,1,0:T(8,128)(2,1)S(1)} %get-tuple-element.35), channel_id=1, source_target_pairs={{0,24},{1,9},{2,26},{3,11},{4,28},{5,13},{6,30},{7,15},{8,0},{9,17... | collective-permute-start | bytes 1032200 | tf_op jit(solution)/shard_map/ppermute | solution.py:39
  24.5 0.0 copy-done.1
  24.6 0.0 collective-permute-done.2
  24.6 1.2 collective-permute-done.3
  25.8 1.7 %collective-permute-done.6 = bf16[3,32,1792]{2,1,0:T(8,128)(2,1)S(1)} collective-permute-done((bf16[3,32,1792]{2,1,0:T(8,128)(2,1)S(1)}, bf16[3,32,1792]{2,1,0:T(8,128)(2,1)S(1)}, u32[]{:S(2)}, u32[]{:S(2)}) %collective-permute-start.6) | collective-permute-done | bytes 344096 | tf_op jit(solution)/shard_map/ppermute | solution.py:39
  27.4 6.5 %collective-permute-done.7 = bf16[3,32,1792]{2,1,0:T(8,128)(2,1)S(1)} collective-permute-done((bf16[3,32,1792]{2,1,0:T(8,128)(2,1)S(1)}, bf16[3,32,1792]{2,1,0:T(8,128)(2,1)S(1)}, u32[]{:S(2)}, u32[]{:S(2)}) %collective-permute-start.7) | collective-permute-done | bytes 344096 | tf_op jit(solution)/shard_map/ppermute | solution.py:39
  33.9 1.4 fusion.4
  35.4 0.0 copy-start.2
  35.4 0.0 copy-start.3
  35.4 1.1 fusion.3
  36.5 6.2 %all-to-all-start = ((bf16[8,3,8,1792]{3,2,1,0:T(8,128)(2,1)}), bf16[8,3,8,1792]{3,2,1,0:T(8,128)(2,1)S(1)}, u32[]{:S(2)}, u32[]{:S(2)}) async-start(bf16[8,3,8,1792]{3,2,1,0:T(8,128)(2,1)} %fusion.3), calls=%async_computation | async-start | bytes 1376256 | tf_op jit(solution)/shard_map/all_to_all | solution.py:119
  42.7 0.0 copy-done.2
  42.7 0.0 copy-done.3
  42.7 14.3 %collective-permute-start = (f32[8,1792]{1,0:T(8,128)S(1)}, f32[8,1792]{1,0:T(8,128)S(1)}, u32[]{:S(2)}, u32[]{:S(2)}) collective-permute-start(f32[8,1792]{1,0:T(8,128)S(1)} %bitcast.107), channel_id=1, source_target_pairs={{0,32},{1,65},{2,34},{3,67},{4,36},{5,69},{6,38},{7,71},{32,64},{3... | collective-permute-start | bytes 172040 | tf_op jit(solution)/shard_map/ppermute | solution.py:39
  57.0 1.9 %collective-permute-start.1 = (f32[8,1792]{1,0:T(8,128)S(1)}, f32[8,1792]{1,0:T(8,128)S(1)}, u32[]{:S(2)}, u32[]{:S(2)}) collective-permute-start(f32[8,1792]{1,0:T(8,128)S(1)} %bitcast.108), channel_id=1, source_target_pairs={{0,64},{1,33},{2,66},{3,35},{4,68},{5,37},{6,70},{7,39},{32,0},{33... | collective-permute-start | bytes 172040 | tf_op jit(solution)/shard_map/ppermute | solution.py:39
  59.0 0.0 collective-permute-done
  59.1 8.6 %collective-permute-done.1 = f32[8,1792]{1,0:T(8,128)S(1)} collective-permute-done((f32[8,1792]{1,0:T(8,128)S(1)}, f32[8,1792]{1,0:T(8,128)S(1)}, u32[]{:S(2)}, u32[]{:S(2)}) %collective-permute-start.1) | collective-permute-done | bytes 57376 | tf_op jit(solution)/shard_map/ppermute | solution.py:39
  67.8 0.0 all-to-all-done
  67.8 0.1 reduce_sum.12
  67.9 10.0 %collective-permute-start.8 = (bf16[3,8,1792]{2,1,0:T(8,128)(2,1)S(1)}, bf16[3,8,1792]{2,1,0:T(8,128)(2,1)S(1)}, u32[]{:S(2)}, u32[]{:S(2)}) collective-permute-start(bf16[3,8,1792]{2,1,0:T(8,128)(2,1)S(1)} %reduce_sum.12), channel_id=1, source_target_pairs={{0,32},{1,65},{2,34},{3,67},{4,36},{5,69},{6,38},{7,71},{32,64},{3... | collective-permute-start | bytes 258056 | tf_op jit(solution)/shard_map/ppermute | solution.py:39
  77.9 1.9 %collective-permute-start.9 = (bf16[3,8,1792]{2,1,0:T(8,128)(2,1)S(1)}, bf16[3,8,1792]{2,1,0:T(8,128)(2,1)S(1)}, u32[]{:S(2)}, u32[]{:S(2)}) collective-permute-start(bf16[3,8,1792]{2,1,0:T(8,128)(2,1)S(1)} %reduce_sum.12), channel_id=1, source_target_pairs={{0,64},{1,33},{2,66},{3,35},{4,68},{5,37},{6,70},{7,39},{32,0},{33... | collective-permute-start | bytes 258056 | tf_op jit(solution)/shard_map/ppermute | solution.py:39
  79.8 0.1 fusion.15
  79.9 0.0 collective-permute-done.8
  79.9 8.5 %collective-permute-done.9 = bf16[3,8,1792]{2,1,0:T(8,128)(2,1)S(1)} collective-permute-done((bf16[3,8,1792]{2,1,0:T(8,128)(2,1)S(1)}, bf16[3,8,1792]{2,1,0:T(8,128)(2,1)S(1)}, u32[]{:S(2)}, u32[]{:S(2)}) %collective-permute-start.9) | collective-permute-done | bytes 86048 | tf_op jit(solution)/shard_map/ppermute | solution.py:39
  88.4 0.1 fusion.17
  88.5 0.9 broadcast_in_dim.59
  89.4 4.9 %all-to-all-start.1 = ((bf16[8,3,8,1792]{3,2,1,0:T(8,128)(2,1)}), bf16[8,3,8,1792]{3,2,1,0:T(8,128)(2,1)S(1)}, u32[]{:S(2)}, u32[]{:S(2)}) async-start(bf16[8,3,8,1792]{3,2,1,0:T(8,128)(2,1)} %broadcast_in_dim.59), calls=%async_computation.1 | async-start | bytes 1376256 | tf_op jit(solution)/shard_map/all_to_all | solution.py:128
  94.3 3.9 %collective-permute-start.16 = (bf16[64,1792]{1,0:T(8,128)(2,1)S(1)}, bf16[64,1792]{1,0:T(8,128)(2,1)S(1)}, u32[]{:S(2)}, u32[]{:S(2)}) collective-permute-start(bf16[64,1792]{1,0:T(8,128)(2,1)S(1)} %get-tuple-element.29), channel_id=1, source_target_pairs={{0,32},{1,65},{2,34},{3,67},{4,36},{5,69},{6,38},{7,71},{32,64},{3... | collective-permute-start | bytes 688136 | tf_op jit(solution)/shard_map/ppermute | solution.py:39
  98.2 5.3 %collective-permute-start.17 = (bf16[64,1792]{1,0:T(8,128)(2,1)S(1)}, bf16[64,1792]{1,0:T(8,128)(2,1)S(1)}, u32[]{:S(2)}, u32[]{:S(2)}) collective-permute-start(bf16[64,1792]{1,0:T(8,128)(2,1)S(1)} %get-tuple-element.30), channel_id=1, source_target_pairs={{0,64},{1,33},{2,66},{3,35},{4,68},{5,37},{6,70},{7,39},{32,0},{33... | collective-permute-start | bytes 688136 | tf_op jit(solution)/shard_map/ppermute | solution.py:39
  103.5 0.6 fusion.19
  104.1 10.7 %all-to-all-done.1 = bf16[8,3,8,1792]{3,2,1,0:T(8,128)(2,1)S(1)} async-done(((bf16[8,3,8,1792]{3,2,1,0:T(8,128)(2,1)}), bf16[8,3,8,1792]{3,2,1,0:T(8,128)(2,1)S(1)}, u32[]{:S(2)}, u32[]{:S(2)}) %all-to-all-start.1) | async-done | bytes 688160 | tf_op jit(solution)/shard_map/all_to_all | solution.py:128
  114.9 1.9 %collective-permute-start.11 = (bf16[3,32,1792]{2,1,0:T(8,128)(2,1)S(1)}, bf16[3,32,1792]{2,1,0:T(8,128)(2,1)S(1)}, u32[]{:S(2)}, u32[]{:S(2)}) collective-permute-start(bf16[3,32,1792]{2,1,0:T(8,128)(2,1)S(1)} %bitcast.104), channel_id=1, source_target_pairs={{0,24},{1,9},{2,26},{3,11},{4,28},{5,13},{6,30},{7,15},{8,0},{9,17... | collective-permute-start | bytes 1032200 | tf_op jit(solution)/shard_map/ppermute | solution.py:39
  116.8 4.6 %collective-permute-start.12 = (bf16[3,32,1792]{2,1,0:T(8,128)(2,1)S(1)}, bf16[3,32,1792]{2,1,0:T(8,128)(2,1)S(1)}, u32[]{:S(2)}, u32[]{:S(2)}) collective-permute-start(bf16[3,32,1792]{2,1,0:T(8,128)(2,1)S(1)} %bitcast.105), channel_id=1, source_target_pairs={{0,8},{1,25},{2,10},{3,27},{4,12},{5,29},{6,14},{7,31},{8,16},{9,1... | collective-permute-start | bytes 1032200 | tf_op jit(solution)/shard_map/ppermute | solution.py:39
  121.5 1.9 %collective-permute-start.10 = (bf16[3,32,1792]{2,1,0:T(8,128)(2,1)S(1)}, bf16[3,32,1792]{2,1,0:T(8,128)(2,1)S(1)}, u32[]{:S(2)}, u32[]{:S(2)}) collective-permute-start(bf16[3,32,1792]{2,1,0:T(8,128)(2,1)S(1)} %bitcast.102), channel_id=1, source_target_pairs={{0,8},{1,25},{2,10},{3,27},{4,12},{5,29},{6,14},{7,31},{8,16},{9,1... | collective-permute-start | bytes 1032200 | tf_op jit(solution)/shard_map/ppermute | solution.py:39
  123.4 0.2 broadcast_in_dim.54
  123.7 7.6 %collective-permute-done.10 = bf16[3,32,1792]{2,1,0:T(8,128)(2,1)S(1)} collective-permute-done((bf16[3,32,1792]{2,1,0:T(8,128)(2,1)S(1)}, bf16[3,32,1792]{2,1,0:T(8,128)(2,1)S(1)}, u32[]{:S(2)}, u32[]{:S(2)}) %collective-permute-start.10) | collective-permute-done | bytes 344096 | tf_op jit(solution)/shard_map/ppermute | solution.py:39
  131.3 1.9 %collective-permute-start.13 = (bf16[3,32,1792]{2,1,0:T(8,128)(2,1)S(1)}, bf16[3,32,1792]{2,1,0:T(8,128)(2,1)S(1)}, u32[]{:S(2)}, u32[]{:S(2)}) collective-permute-start(bf16[3,32,1792]{2,1,0:T(8,128)(2,1)S(1)} %bitcast.103), channel_id=1, source_target_pairs={{0,24},{1,9},{2,26},{3,11},{4,28},{5,13},{6,30},{7,15},{8,0},{9,17... | collective-permute-start | bytes 1032200 | tf_op jit(solution)/shard_map/ppermute | solution.py:39
  133.3 0.0 collective-permute-done.11
  133.3 4.6 %collective-permute-start.14 = (bf16[3,32,1792]{2,1,0:T(8,128)(2,1)S(1)}, bf16[3,32,1792]{2,1,0:T(8,128)(2,1)S(1)}, u32[]{:S(2)}, u32[]{:S(2)}) collective-permute-start(bf16[3,32,1792]{2,1,0:T(8,128)(2,1)S(1)} %collective-permute-done.10), channel_id=1, source_target_pairs={{0,8},{1,25},{2,10},{3,27},{4,12},{5,29},{6,14},{7,31},{8,16},{9,1... | collective-permute-start | bytes 1032200 | tf_op jit(solution)/shard_map/ppermute | solution.py:39
  137.9 0.0 collective-permute-done.12
  137.9 1.9 %collective-permute-start.15 = (bf16[3,32,1792]{2,1,0:T(8,128)(2,1)S(1)}, bf16[3,32,1792]{2,1,0:T(8,128)(2,1)S(1)}, u32[]{:S(2)}, u32[]{:S(2)}) collective-permute-start(bf16[3,32,1792]{2,1,0:T(8,128)(2,1)S(1)} %collective-permute-done.11), channel_id=1, source_target_pairs={{0,24},{1,9},{2,26},{3,11},{4,28},{5,13},{6,30},{7,15},{8,0},{9,17... | collective-permute-start | bytes 1032200 | tf_op jit(solution)/shard_map/ppermute | solution.py:39
  139.9 1.3 collective-permute-done.13
  141.2 0.0 collective-permute-done.16
  141.3 0.0 collective-permute-done.17
  141.3 4.0 %collective-permute-done.14 = bf16[3,32,1792]{2,1,0:T(8,128)(2,1)S(1)} collective-permute-done((bf16[3,32,1792]{2,1,0:T(8,128)(2,1)S(1)}, bf16[3,32,1792]{2,1,0:T(8,128)(2,1)S(1)}, u32[]{:S(2)}, u32[]{:S(2)}) %collective-permute-start.14) | collective-permute-done | bytes 344096 | tf_op jit(solution)/shard_map/ppermute | solution.py:39
  145.3 0.9 fusion.14
  146.2 1.7 %collective-permute-done.15 = bf16[3,32,1792]{2,1,0:T(8,128)(2,1)S(1)} collective-permute-done((bf16[3,32,1792]{2,1,0:T(8,128)(2,1)S(1)}, bf16[3,32,1792]{2,1,0:T(8,128)(2,1)S(1)}, u32[]{:S(2)}, u32[]{:S(2)}) %collective-permute-start.15) | collective-permute-done | bytes 344096 | tf_op jit(solution)/shard_map/ppermute | solution.py:39
  147.9 0.0 copy-start
  147.9 1.5 %copy-done = bf16[3,4,64,1792]{3,2,1,0:T(8,128)(2,1)} copy-done((bf16[3,4,64,1792]{3,2,1,0:T(8,128)(2,1)}, bf16[3,4,64,1792]{3,2,1,0:T(8,128)(2,1)S(1)}, u32[]{:S(2)}) %copy-start) | copy-done | bytes 2752536
  (18 shorter events, 0.5 us)
Async XLA Ops:
  0.6 23.9 %copy-start.1 = (f32[1,64,1792]{2,1,0:T(8,128)S(1)}, f32[1,64,1792]{2,1,0:T(8,128)}, u32[]{:S(2)}) copy-start(f32[1,64,1792]{2,1,0:T(8,128)} %param.5) | copy-start | bytes 1376260
  1.9 14.9 %collective-permute-start.4 = (bf16[3,32,1792]{2,1,0:T(8,128)(2,1)S(1)}, bf16[3,32,1792]{2,1,0:T(8,128)(2,1)S(1)}, u32[]{:S(2)}, u32[]{:S(2)}) collective-permute-start(bf16[3,32,1792]{2,1,0:T(8,128)(2,1)S(1)} %get-tuple-element.19), channel_id=1, source_target_pairs={{0,8},{1,25},{2,10},{3,27},{4,12},{5,29},{6,14},{7,31},{8,16},{9,1... | collective-permute-start | bytes 1032200 | tf_op jit(solution)/shard_map/ppermute | solution.py:39
  7.1 9.7 %collective-permute-start.5 = (bf16[3,32,1792]{2,1,0:T(8,128)(2,1)S(1)}, bf16[3,32,1792]{2,1,0:T(8,128)(2,1)S(1)}, u32[]{:S(2)}, u32[]{:S(2)}) collective-permute-start(bf16[3,32,1792]{2,1,0:T(8,128)(2,1)S(1)} %get-tuple-element.20), channel_id=1, source_target_pairs={{0,24},{1,9},{2,26},{3,11},{4,28},{5,13},{6,30},{7,15},{8,0},{9,17... | collective-permute-start | bytes 1032200 | tf_op jit(solution)/shard_map/ppermute | solution.py:39
  10.2 14.4 %collective-permute-start.2 = (bf16[3,32,1792]{2,1,0:T(8,128)(2,1)S(1)}, bf16[3,32,1792]{2,1,0:T(8,128)(2,1)S(1)}, u32[]{:S(2)}, u32[]{:S(2)}) collective-permute-start(bf16[3,32,1792]{2,1,0:T(8,128)(2,1)S(1)} %get-tuple-element.38), channel_id=1, source_target_pairs={{0,8},{1,25},{2,10},{3,27},{4,12},{5,29},{6,14},{7,31},{8,16},{9,1... | collective-permute-start | bytes 1032200 | tf_op jit(solution)/shard_map/ppermute | solution.py:39
  14.8 11.0 %collective-permute-start.3 = (bf16[3,32,1792]{2,1,0:T(8,128)(2,1)S(1)}, bf16[3,32,1792]{2,1,0:T(8,128)(2,1)}, u32[]{:S(2)}, u32[]{:S(2)}) collective-permute-start(bf16[3,32,1792]{2,1,0:T(8,128)(2,1)S(1)} %get-tuple-element.37), channel_id=1, source_target_pairs={{0,24},{1,9},{2,26},{3,11},{4,28},{5,13},{6,30},{7,15},{8,0},{9,17... | collective-permute-start | bytes 1032200 | tf_op jit(solution)/shard_map/ppermute | solution.py:39
  18.0 9.4 %collective-permute-start.6 = (bf16[3,32,1792]{2,1,0:T(8,128)(2,1)S(1)}, bf16[3,32,1792]{2,1,0:T(8,128)(2,1)S(1)}, u32[]{:S(2)}, u32[]{:S(2)}) collective-permute-start(bf16[3,32,1792]{2,1,0:T(8,128)(2,1)S(1)} %get-tuple-element.36), channel_id=1, source_target_pairs={{0,8},{1,25},{2,10},{3,27},{4,12},{5,29},{6,14},{7,31},{8,16},{9,1... | collective-permute-start | bytes 1032200 | tf_op jit(solution)/shard_map/ppermute | solution.py:39
  22.6 11.4 %collective-permute-start.7 = (bf16[3,32,1792]{2,1,0:T(8,128)(2,1)S(1)}, bf16[3,32,1792]{2,1,0:T(8,128)(2,1)S(1)}, u32[]{:S(2)}, u32[]{:S(2)}) collective-permute-start(bf16[3,32,1792]{2,1,0:T(8,128)(2,1)S(1)} %get-tuple-element.35), channel_id=1, source_target_pairs={{0,24},{1,9},{2,26},{3,11},{4,28},{5,13},{6,30},{7,15},{8,0},{9,17... | collective-permute-start | bytes 1032200 | tf_op jit(solution)/shard_map/ppermute | solution.py:39
  35.4 7.3 %copy-start.2 = (f32[1,8,1792]{2,1,0:T(8,128)S(1)}, f32[1,8,1792]{2,1,0:T(8,128)}, u32[]{:S(2)}) copy-start(f32[1,8,1792]{2,1,0:T(8,128)} %param.6) | copy-start | bytes 172036
  35.4 7.3 %copy-start.3 = (f32[1,8,1792]{2,1,0:T(8,128)S(1)}, f32[1,8,1792]{2,1,0:T(8,128)}, u32[]{:S(2)}) copy-start(f32[1,8,1792]{2,1,0:T(8,128)} %param.7) | copy-start | bytes 172036
  36.5 31.3 %all-to-all-start = ((bf16[8,3,8,1792]{3,2,1,0:T(8,128)(2,1)}), bf16[8,3,8,1792]{3,2,1,0:T(8,128)(2,1)S(1)}, u32[]{:S(2)}, u32[]{:S(2)}) async-start(bf16[8,3,8,1792]{3,2,1,0:T(8,128)(2,1)} %fusion.3), calls=%async_computation | async-start | bytes 1376256 | tf_op jit(solution)/shard_map/all_to_all | solution.py:119
  42.7 16.3 %collective-permute-start = (f32[8,1792]{1,0:T(8,128)S(1)}, f32[8,1792]{1,0:T(8,128)S(1)}, u32[]{:S(2)}, u32[]{:S(2)}) collective-permute-start(f32[8,1792]{1,0:T(8,128)S(1)} %bitcast.107), channel_id=1, source_target_pairs={{0,32},{1,65},{2,34},{3,67},{4,36},{5,69},{6,38},{7,71},{32,64},{3... | collective-permute-start | bytes 172040 | tf_op jit(solution)/shard_map/ppermute | solution.py:39
  57.0 10.7 %collective-permute-start.1 = (f32[8,1792]{1,0:T(8,128)S(1)}, f32[8,1792]{1,0:T(8,128)S(1)}, u32[]{:S(2)}, u32[]{:S(2)}) collective-permute-start(f32[8,1792]{1,0:T(8,128)S(1)} %bitcast.108), channel_id=1, source_target_pairs={{0,64},{1,33},{2,66},{3,35},{4,68},{5,37},{6,70},{7,39},{32,0},{33... | collective-permute-start | bytes 172040 | tf_op jit(solution)/shard_map/ppermute | solution.py:39
  67.9 12.0 %collective-permute-start.8 = (bf16[3,8,1792]{2,1,0:T(8,128)(2,1)S(1)}, bf16[3,8,1792]{2,1,0:T(8,128)(2,1)S(1)}, u32[]{:S(2)}, u32[]{:S(2)}) collective-permute-start(bf16[3,8,1792]{2,1,0:T(8,128)(2,1)S(1)} %reduce_sum.12), channel_id=1, source_target_pairs={{0,32},{1,65},{2,34},{3,67},{4,36},{5,69},{6,38},{7,71},{32,64},{3... | collective-permute-start | bytes 258056 | tf_op jit(solution)/shard_map/ppermute | solution.py:39
  77.9 10.5 %collective-permute-start.9 = (bf16[3,8,1792]{2,1,0:T(8,128)(2,1)S(1)}, bf16[3,8,1792]{2,1,0:T(8,128)(2,1)S(1)}, u32[]{:S(2)}, u32[]{:S(2)}) collective-permute-start(bf16[3,8,1792]{2,1,0:T(8,128)(2,1)S(1)} %reduce_sum.12), channel_id=1, source_target_pairs={{0,64},{1,33},{2,66},{3,35},{4,68},{5,37},{6,70},{7,39},{32,0},{33... | collective-permute-start | bytes 258056 | tf_op jit(solution)/shard_map/ppermute | solution.py:39
  89.4 25.4 %all-to-all-start.1 = ((bf16[8,3,8,1792]{3,2,1,0:T(8,128)(2,1)}), bf16[8,3,8,1792]{3,2,1,0:T(8,128)(2,1)S(1)}, u32[]{:S(2)}, u32[]{:S(2)}) async-start(bf16[8,3,8,1792]{3,2,1,0:T(8,128)(2,1)} %broadcast_in_dim.59), calls=%async_computation.1 | async-start | bytes 1376256 | tf_op jit(solution)/shard_map/all_to_all | solution.py:128
  94.3 47.0 %collective-permute-start.16 = (bf16[64,1792]{1,0:T(8,128)(2,1)S(1)}, bf16[64,1792]{1,0:T(8,128)(2,1)S(1)}, u32[]{:S(2)}, u32[]{:S(2)}) collective-permute-start(bf16[64,1792]{1,0:T(8,128)(2,1)S(1)} %get-tuple-element.29), channel_id=1, source_target_pairs={{0,32},{1,65},{2,34},{3,67},{4,36},{5,69},{6,38},{7,71},{32,64},{3... | collective-permute-start | bytes 688136 | tf_op jit(solution)/shard_map/ppermute | solution.py:39
  98.2 43.1 %collective-permute-start.17 = (bf16[64,1792]{1,0:T(8,128)(2,1)S(1)}, bf16[64,1792]{1,0:T(8,128)(2,1)S(1)}, u32[]{:S(2)}, u32[]{:S(2)}) collective-permute-start(bf16[64,1792]{1,0:T(8,128)(2,1)S(1)} %get-tuple-element.30), channel_id=1, source_target_pairs={{0,64},{1,33},{2,66},{3,35},{4,68},{5,37},{6,70},{7,39},{32,0},{33... | collective-permute-start | bytes 688136 | tf_op jit(solution)/shard_map/ppermute | solution.py:39
  114.9 18.4 %collective-permute-start.11 = (bf16[3,32,1792]{2,1,0:T(8,128)(2,1)S(1)}, bf16[3,32,1792]{2,1,0:T(8,128)(2,1)S(1)}, u32[]{:S(2)}, u32[]{:S(2)}) collective-permute-start(bf16[3,32,1792]{2,1,0:T(8,128)(2,1)S(1)} %bitcast.104), channel_id=1, source_target_pairs={{0,24},{1,9},{2,26},{3,11},{4,28},{5,13},{6,30},{7,15},{8,0},{9,17... | collective-permute-start | bytes 1032200 | tf_op jit(solution)/shard_map/ppermute | solution.py:39
  116.8 21.1 %collective-permute-start.12 = (bf16[3,32,1792]{2,1,0:T(8,128)(2,1)S(1)}, bf16[3,32,1792]{2,1,0:T(8,128)(2,1)S(1)}, u32[]{:S(2)}, u32[]{:S(2)}) collective-permute-start(bf16[3,32,1792]{2,1,0:T(8,128)(2,1)S(1)} %bitcast.105), channel_id=1, source_target_pairs={{0,8},{1,25},{2,10},{3,27},{4,12},{5,29},{6,14},{7,31},{8,16},{9,1... | collective-permute-start | bytes 1032200 | tf_op jit(solution)/shard_map/ppermute | solution.py:39
  121.5 9.9 %collective-permute-start.10 = (bf16[3,32,1792]{2,1,0:T(8,128)(2,1)S(1)}, bf16[3,32,1792]{2,1,0:T(8,128)(2,1)S(1)}, u32[]{:S(2)}, u32[]{:S(2)}) collective-permute-start(bf16[3,32,1792]{2,1,0:T(8,128)(2,1)S(1)} %bitcast.102), channel_id=1, source_target_pairs={{0,8},{1,25},{2,10},{3,27},{4,12},{5,29},{6,14},{7,31},{8,16},{9,1... | collective-permute-start | bytes 1032200 | tf_op jit(solution)/shard_map/ppermute | solution.py:39
  131.3 9.9 %collective-permute-start.13 = (bf16[3,32,1792]{2,1,0:T(8,128)(2,1)S(1)}, bf16[3,32,1792]{2,1,0:T(8,128)(2,1)S(1)}, u32[]{:S(2)}, u32[]{:S(2)}) collective-permute-start(bf16[3,32,1792]{2,1,0:T(8,128)(2,1)S(1)} %bitcast.103), channel_id=1, source_target_pairs={{0,24},{1,9},{2,26},{3,11},{4,28},{5,13},{6,30},{7,15},{8,0},{9,17... | collective-permute-start | bytes 1032200 | tf_op jit(solution)/shard_map/ppermute | solution.py:39
  133.3 12.0 %collective-permute-start.14 = (bf16[3,32,1792]{2,1,0:T(8,128)(2,1)S(1)}, bf16[3,32,1792]{2,1,0:T(8,128)(2,1)S(1)}, u32[]{:S(2)}, u32[]{:S(2)}) collective-permute-start(bf16[3,32,1792]{2,1,0:T(8,128)(2,1)S(1)} %collective-permute-done.10), channel_id=1, source_target_pairs={{0,8},{1,25},{2,10},{3,27},{4,12},{5,29},{6,14},{7,31},{8,16},{9,1... | collective-permute-start | bytes 1032200 | tf_op jit(solution)/shard_map/ppermute | solution.py:39
  137.9 10.0 %collective-permute-start.15 = (bf16[3,32,1792]{2,1,0:T(8,128)(2,1)S(1)}, bf16[3,32,1792]{2,1,0:T(8,128)(2,1)S(1)}, u32[]{:S(2)}, u32[]{:S(2)}) collective-permute-start(bf16[3,32,1792]{2,1,0:T(8,128)(2,1)S(1)} %collective-permute-done.11), channel_id=1, source_target_pairs={{0,24},{1,9},{2,26},{3,11},{4,28},{5,13},{6,30},{7,15},{8,0},{9,17... | collective-permute-start | bytes 1032200 | tf_op jit(solution)/shard_map/ppermute | solution.py:39
  147.9 1.5 %copy-start = (bf16[3,4,64,1792]{3,2,1,0:T(8,128)(2,1)}, bf16[3,4,64,1792]{3,2,1,0:T(8,128)(2,1)S(1)}, u32[]{:S(2)}) copy-start(bf16[3,4,64,1792]{3,2,1,0:T(8,128)(2,1)S(1)} %bitcast_dynamic-update-slice_fusion) | copy-start | bytes 8257540

commit v2 on v0

--- a/solution.py
+++ b/solution.py
@@ -46,11 +46,12 @@
     onward, back = lax.optimization_barrier((onward, back))
     onward = tagged(narrow(wide(block(own, up, 0)) + wide(onward)), 1)
     back = tagged(narrow(wide(block(own, down, 1)) + wide(back)), 3)
-    parts = (from_down, from_up, onward, back)
-    from_down, from_up, onward, back = lax.optimization_barrier(parts)
+    parts = (own, from_down, from_up, onward)
+    own, from_down, from_up, onward = lax.optimization_barrier(parts)
     first = wide(block(own, m, 0)) + wide(from_up) + wide(onward)
-    second = wide(block(own, m, 1)) + wide(from_down) + wide(back)
-    return jnp.concatenate((first, second), axis=1)
+    second = wide(block(own, m, 1)) + wide(from_down)
+    first, second, back = lax.optimization_barrier((first, second, back))
+    return jnp.concatenate((first, second + wide(back)), axis=1)
 
 
 def x_gather(rows, m):

time: 145 us -> 148 us (1.021)
  the two profiles are of different devices: /device:TPU:198 before, /device:TPU:192 now
where the time goes in v2:
time: 148 us; the launch traced here: 147 us
  starting transfers between devices  89.9 us (61%)
  waiting for transfers between devices  43.4 us (29%)
  local copies, waits for them, and re-layouts  7.19 us (5%)
  other arithmetic  5.54 us (4%)
    ppermute x18, starting transfers between devices, turn(): return lax.ppermute(x, axis, [(k, (k + step) % n) for k in range(n)])  77.3 us
    ppermute x18, waiting for transfers between devices, turn(): return lax.ppermute(x, axis, [(k, (k + step) % n) for k in range(n)])  38.2 us
    all_to_all x1, starting transfers between devices, step(): blocks = lax.all_to_all(blocks, 'outer', 0, 0, tiled=True)  7.1 us
    all_to_all x1, starting transfers between devices, step(): rows = lax.all_to_all(copies, 'outer', 0, 0, tiled=True)  5.54 us
    all_to_all x1, waiting for transfers between devices, step(): rows = lax.all_to_all(copies, 'outer', 0, 0, tiled=True)  5.25 us
    squeeze x2, local copies, waits for them, and re-layouts, block(): lax.dynamic_slice(own, (0, k, h * half, 0), (n, 1, half, columns))[:, 0]  4.14 us
  transfers between devices with their start and end apart: 20, of which 10 were waited for; matrix products, arithmetic and copies ran while one was open for 5% of the time, Pallas kernels for 0%

profile of v2, /device:TPU:192, one launch (start us, length us, event | category | flops | bytes accessed | tf_op | source)
XLA Modules:
  0.0 147.3 jit_solution(3263747790603330477)
XLA Ops:
  0.6 0.0 copy-start
  0.6 0.0 copy-start.2
  0.7 2.2 %dynamic-slice_bitcast_fusion.2 = (bf16[3,32,1792]{2,1,0:T(8,128)(2,1)}, bf16[3,32,1792]{2,1,0:T(8,128)(2,1)}) fusion(bf16[3,4,64,1792]{3,2,1,0:T(8,128)(2,1)} %bitcast.97, s32[]{:T(128)S(6)} %select_n.108), kind=kLoop, calls=%fused_computation.39 | loop fusion | bytes 1376260 | tf_op jit(solution)/shard_map/squeeze | solution.py:31
  2.8 3.4 %collective-permute-start.4 = (bf16[3,32,1792]{2,1,0:T(8,128)(2,1)}, bf16[3,32,1792]{2,1,0:T(8,128)(2,1)}, u32[]{:S(2)}, u32[]{:S(2)}) collective-permute-start(bf16[3,32,1792]{2,1,0:T(8,128)(2,1)} %get-tuple-element.22), channel_id=1, source_target_pairs={{0,8},{8,16},{16,24},{24,0},{1,9},{9,17},{17,25},{25,1},{2,10},{10... | collective-permute-start | bytes 1032200 | tf_op jit(solution)/shard_map/ppermute | solution.py:25
  6.2 3.7 %collective-permute-start.5 = (bf16[3,32,1792]{2,1,0:T(8,128)(2,1)}, bf16[3,32,1792]{2,1,0:T(8,128)(2,1)}, u32[]{:S(2)}, u32[]{:S(2)}) collective-permute-start(bf16[3,32,1792]{2,1,0:T(8,128)(2,1)} %get-tuple-element.23), channel_id=1, source_target_pairs={{0,24},{8,0},{16,8},{24,16},{1,25},{9,1},{17,9},{25,17},{2,26},{10... | collective-permute-start | bytes 1032200 | tf_op jit(solution)/shard_map/ppermute | solution.py:25
  9.9 2.0 %dynamic-slice_bitcast_fusion = (bf16[3,32,1792]{2,1,0:T(8,128)(2,1)}, bf16[3,32,1792]{2,1,0:T(8,128)(2,1)}) fusion(bf16[3,4,64,1792]{3,2,1,0:T(8,128)(2,1)} %bitcast.98, s32[]{:T(128)S(6)} %select_n.112, s32[]{:T(128)S(6)} %select_n.110), kind=kLoop, calls=%fused_computation.37 | loop fusion | bytes 1376264 | tf_op jit(solution)/shard_map/squeeze | solution.py:31
  11.9 2.2 %collective-permute-start.2 = (bf16[3,32,1792]{2,1,0:T(8,128)(2,1)}, bf16[3,32,1792]{2,1,0:T(8,128)(2,1)}, u32[]{:S(2)}, u32[]{:S(2)}) collective-permute-start(bf16[3,32,1792]{2,1,0:T(8,128)(2,1)} %get-tuple-element.44), channel_id=1, source_target_pairs={{0,8},{8,16},{16,24},{24,0},{1,9},{9,17},{17,25},{25,1},{2,10},{10... | collective-permute-start | bytes 1032200 | tf_op jit(solution)/shard_map/ppermute | solution.py:25
  14.1 4.9 %collective-permute-start.3 = (bf16[3,32,1792]{2,1,0:T(8,128)(2,1)}, bf16[3,32,1792]{2,1,0:T(8,128)(2,1)}, u32[]{:S(2)}, u32[]{:S(2)}) collective-permute-start(bf16[3,32,1792]{2,1,0:T(8,128)(2,1)} %get-tuple-element.43), channel_id=1, source_target_pairs={{0,24},{8,0},{16,8},{24,16},{1,25},{9,1},{17,9},{25,17},{2,26},{10... | collective-permute-start | bytes 1032200 | tf_op jit(solution)/shard_map/ppermute | solution.py:25
  19.0 0.0 collective-permute-done.4
  19.0 0.0 collective-permute-done.5
  19.0 0.0 copy-done
  19.0 1.2 fusion.4
  20.3 2.4 %collective-permute-start.6 = (bf16[3,32,1792]{2,1,0:T(8,128)(2,1)S(1)}, bf16[3,32,1792]{2,1,0:T(8,128)(2,1)S(1)}, u32[]{:S(2)}, u32[]{:S(2)}) collective-permute-start(bf16[3,32,1792]{2,1,0:T(8,128)(2,1)S(1)} %get-tuple-element.42), channel_id=1, source_target_pairs={{0,8},{8,16},{16,24},{24,0},{1,9},{9,17},{17,25},{25,1},{2,10},{10... | collective-permute-start | bytes 1032200 | tf_op jit(solution)/shard_map/ppermute | solution.py:25
  22.7 0.0 copy-done.2
  22.7 4.6 %collective-permute-start.7 = (bf16[3,32,1792]{2,1,0:T(8,128)(2,1)S(1)}, bf16[3,32,1792]{2,1,0:T(8,128)(2,1)S(1)}, u32[]{:S(2)}, u32[]{:S(2)}) collective-permute-start(bf16[3,32,1792]{2,1,0:T(8,128)(2,1)S(1)} %get-tuple-element.41), channel_id=1, source_target_pairs={{0,24},{8,0},{16,8},{24,16},{1,25},{9,1},{17,9},{25,17},{2,26},{10... | collective-permute-start | bytes 1032200 | tf_op jit(solution)/shard_map/ppermute | solution.py:25
  27.4 0.0 collective-permute-done.2
  27.4 0.0 collective-permute-done.3
  27.4 4.6 %collective-permute-done.6 = bf16[3,32,1792]{2,1,0:T(8,128)(2,1)S(1)} collective-permute-done((bf16[3,32,1792]{2,1,0:T(8,128)(2,1)S(1)}, bf16[3,32,1792]{2,1,0:T(8,128)(2,1)S(1)}, u32[]{:S(2)}, u32[]{:S(2)}) %collective-permute-start.6) | collective-permute-done | bytes 344096 | tf_op jit(solution)/shard_map/ppermute | solution.py:25
  32.1 1.3 convert_add_fusion.1
  33.3 0.0 collective-permute-done.7
  33.3 0.0 copy-start.4
  33.3 0.0 copy-start.5
  33.4 0.1 convert_add_fusion.4
  33.4 1.1 fusion.3
  34.5 7.1 %all-to-all-start = ((bf16[8,3,8,1792]{3,2,1,0:T(8,128)(2,1)}), bf16[8,3,8,1792]{3,2,1,0:T(8,128)(2,1)S(1)}, u32[]{:S(2)}, u32[]{:S(2)}) async-start(bf16[8,3,8,1792]{3,2,1,0:T(8,128)(2,1)} %fusion.3), calls=%async_computation | async-start | bytes 1376256 | tf_op jit(solution)/shard_map/all_to_all | solution.py:105
  41.6 0.0 copy-done.4
  41.6 0.0 copy-done.5
  41.6 10.6 %collective-permute-start = (f32[8,1792]{1,0:T(8,128)S(1)}, f32[8,1792]{1,0:T(8,128)S(1)}, u32[]{:S(2)}, u32[]{:S(2)}) collective-permute-start(f32[8,1792]{1,0:T(8,128)S(1)} %bitcast.107), channel_id=1, source_target_pairs={{0,32},{32,64},{64,0},{1,33},{33,65},{65,1},{2,34},{34,66},{66,2},... | collective-permute-start | bytes 172040 | tf_op jit(solution)/shard_map/ppermute | solution.py:25
  52.3 3.2 %collective-permute-start.1 = (f32[8,1792]{1,0:T(8,128)S(1)}, f32[8,1792]{1,0:T(8,128)S(1)}, u32[]{:S(2)}, u32[]{:S(2)}) collective-permute-start(f32[8,1792]{1,0:T(8,128)S(1)} %bitcast.108), channel_id=1, source_target_pairs={{0,64},{32,0},{64,32},{1,65},{33,1},{65,33},{2,66},{34,2},{66,34},... | collective-permute-start | bytes 172040 | tf_op jit(solution)/shard_map/ppermute | solution.py:25
  55.5 1.9 %collective-permute-done = f32[8,1792]{1,0:T(8,128)S(1)} collective-permute-done((f32[8,1792]{1,0:T(8,128)S(1)}, f32[8,1792]{1,0:T(8,128)S(1)}, u32[]{:S(2)}, u32[]{:S(2)}) %collective-permute-start) | collective-permute-done | bytes 57376 | tf_op jit(solution)/shard_map/ppermute | solution.py:25
  57.5 4.8 %collective-permute-done.1 = f32[8,1792]{1,0:T(8,128)S(1)} collective-permute-done((f32[8,1792]{1,0:T(8,128)S(1)}, f32[8,1792]{1,0:T(8,128)S(1)}, u32[]{:S(2)}, u32[]{:S(2)}) %collective-permute-start.1) | collective-permute-done | bytes 57376 | tf_op jit(solution)/shard_map/ppermute | solution.py:25
  62.3 0.0 all-to-all-done
  62.4 0.1 reduce_sum.12
  62.5 8.9 %collective-permute-start.8 = (bf16[3,8,1792]{2,1,0:T(8,128)(2,1)S(1)}, bf16[3,8,1792]{2,1,0:T(8,128)(2,1)S(1)}, u32[]{:S(2)}, u32[]{:S(2)}) collective-permute-start(bf16[3,8,1792]{2,1,0:T(8,128)(2,1)S(1)} %reduce_sum.12), channel_id=1, source_target_pairs={{0,32},{32,64},{64,0},{1,33},{33,65},{65,1},{2,34},{34,66},{66,2},... | collective-permute-start | bytes 258056 | tf_op jit(solution)/shard_map/ppermute | solution.py:25
  71.4 3.2 %collective-permute-start.9 = (bf16[3,8,1792]{2,1,0:T(8,128)(2,1)S(1)}, bf16[3,8,1792]{2,1,0:T(8,128)(2,1)S(1)}, u32[]{:S(2)}, u32[]{:S(2)}) collective-permute-start(bf16[3,8,1792]{2,1,0:T(8,128)(2,1)S(1)} %reduce_sum.12), channel_id=1, source_target_pairs={{0,64},{32,0},{64,32},{1,65},{33,1},{65,33},{2,66},{34,2},{66,34},... | collective-permute-start | bytes 258056 | tf_op jit(solution)/shard_map/ppermute | solution.py:25
  74.6 0.1 fusion.14
  74.6 3.4 %collective-permute-done.8 = bf16[3,8,1792]{2,1,0:T(8,128)(2,1)S(1)} collective-permute-done((bf16[3,8,1792]{2,1,0:T(8,128)(2,1)S(1)}, bf16[3,8,1792]{2,1,0:T(8,128)(2,1)S(1)}, u32[]{:S(2)}, u32[]{:S(2)}) %collective-permute-start.8) | collective-permute-done | bytes 86048 | tf_op jit(solution)/shard_map/ppermute | solution.py:25
  78.0 3.7 %collective-permute-done.9 = bf16[3,8,1792]{2,1,0:T(8,128)(2,1)S(1)} collective-permute-done((bf16[3,8,1792]{2,1,0:T(8,128)(2,1)S(1)}, bf16[3,8,1792]{2,1,0:T(8,128)(2,1)S(1)}, u32[]{:S(2)}, u32[]{:S(2)}) %collective-permute-start.9) | collective-permute-done | bytes 86048 | tf_op jit(solution)/shard_map/ppermute | solution.py:25
  81.7 0.1 fusion.16
  81.8 0.9 broadcast_in_dim.59
  82.7 5.5 %all-to-all-start.1 = ((bf16[8,3,8,1792]{3,2,1,0:T(8,128)(2,1)}), bf16[8,3,8,1792]{3,2,1,0:T(8,128)(2,1)S(1)}, u32[]{:S(2)}, u32[]{:S(2)}) async-start(bf16[8,3,8,1792]{3,2,1,0:T(8,128)(2,1)} %broadcast_in_dim.59), calls=%async_computation.1 | async-start | bytes 1376256 | tf_op jit(solution)/shard_map/all_to_all | solution.py:114
  88.2 4.2 %collective-permute-start.16 = (bf16[64,1792]{1,0:T(8,128)(2,1)S(1)}, bf16[64,1792]{1,0:T(8,128)(2,1)S(1)}, u32[]{:S(2)}, u32[]{:S(2)}) collective-permute-start(bf16[64,1792]{1,0:T(8,128)(2,1)S(1)} %get-tuple-element.35), channel_id=1, source_target_pairs={{0,32},{32,64},{64,0},{1,33},{33,65},{65,1},{2,34},{34,66},{66,2},... | collective-permute-start | bytes 688136 | tf_op jit(solution)/shard_map/ppermute | solution.py:25
  92.5 5.5 %collective-permute-start.17 = (bf16[64,1792]{1,0:T(8,128)(2,1)S(1)}, bf16[64,1792]{1,0:T(8,128)(2,1)S(1)}, u32[]{:S(2)}, u32[]{:S(2)}) collective-permute-start(bf16[64,1792]{1,0:T(8,128)(2,1)S(1)} %get-tuple-element.36), channel_id=1, source_target_pairs={{0,64},{32,0},{64,32},{1,65},{33,1},{65,33},{2,66},{34,2},{66,34},... | collective-permute-start | bytes 688136 | tf_op jit(solution)/shard_map/ppermute | solution.py:25
  98.0 0.6 fusion.18
  98.6 5.2 %all-to-all-done.1 = bf16[8,3,8,1792]{3,2,1,0:T(8,128)(2,1)S(1)} async-done(((bf16[8,3,8,1792]{3,2,1,0:T(8,128)(2,1)}), bf16[8,3,8,1792]{3,2,1,0:T(8,128)(2,1)S(1)}, u32[]{:S(2)}, u32[]{:S(2)}) %all-to-all-start.1) | async-done | bytes 688160 | tf_op jit(solution)/shard_map/all_to_all | solution.py:114
  104.0 7.7 %collective-permute-start.11 = (bf16[3,32,1792]{2,1,0:T(8,128)(2,1)S(1)}, bf16[3,32,1792]{2,1,0:T(8,128)(2,1)S(1)}, u32[]{:S(2)}, u32[]{:S(2)}) collective-permute-start(bf16[3,32,1792]{2,1,0:T(8,128)(2,1)S(1)} %bitcast.104), channel_id=1, source_target_pairs={{0,24},{8,0},{16,8},{24,16},{1,25},{9,1},{17,9},{25,17},{2,26},{10... | collective-permute-start | bytes 1032200 | tf_op jit(solution)/shard_map/ppermute | solution.py:25
  111.7 1.9 %collective-permute-start.12 = (bf16[3,32,1792]{2,1,0:T(8,128)(2,1)S(1)}, bf16[3,32,1792]{2,1,0:T(8,128)(2,1)S(1)}, u32[]{:S(2)}, u32[]{:S(2)}) collective-permute-start(bf16[3,32,1792]{2,1,0:T(8,128)(2,1)S(1)} %bitcast.105), channel_id=1, source_target_pairs={{0,8},{8,16},{16,24},{24,0},{1,9},{9,17},{17,25},{25,1},{2,10},{10... | collective-permute-start | bytes 1032200 | tf_op jit(solution)/shard_map/ppermute | solution.py:25
  113.6 1.9 %collective-permute-start.10 = (bf16[3,32,1792]{2,1,0:T(8,128)(2,1)S(1)}, bf16[3,32,1792]{2,1,0:T(8,128)(2,1)S(1)}, u32[]{:S(2)}, u32[]{:S(2)}) collective-permute-start(bf16[3,32,1792]{2,1,0:T(8,128)(2,1)S(1)} %bitcast.102), channel_id=1, source_target_pairs={{0,8},{8,16},{16,24},{24,0},{1,9},{9,17},{17,25},{25,1},{2,10},{10... | collective-permute-start | bytes 1032200 | tf_op jit(solution)/shard_map/ppermute | solution.py:25
  115.6 0.2 broadcast_in_dim.54
  115.8 0.0 copy-start.3
  115.9 13.3 %collective-permute-done.10 = bf16[3,32,1792]{2,1,0:T(8,128)(2,1)S(1)} collective-permute-done((bf16[3,32,1792]{2,1,0:T(8,128)(2,1)S(1)}, bf16[3,32,1792]{2,1,0:T(8,128)(2,1)S(1)}, u32[]{:S(2)}, u32[]{:S(2)}) %collective-permute-start.10) | collective-permute-done | bytes 344096 | tf_op jit(solution)/shard_map/ppermute | solution.py:25
  129.2 1.9 %collective-permute-start.13 = (bf16[3,32,1792]{2,1,0:T(8,128)(2,1)S(1)}, bf16[3,32,1792]{2,1,0:T(8,128)(2,1)S(1)}, u32[]{:S(2)}, u32[]{:S(2)}) collective-permute-start(bf16[3,32,1792]{2,1,0:T(8,128)(2,1)S(1)} %bitcast.103), channel_id=1, source_target_pairs={{0,24},{8,0},{16,8},{24,16},{1,25},{9,1},{17,9},{25,17},{2,26},{10... | collective-permute-start | bytes 1032200 | tf_op jit(solution)/shard_map/ppermute | solution.py:25
  131.2 0.0 collective-permute-done.11
  131.2 3.9 %collective-permute-start.14 = (bf16[3,32,1792]{2,1,0:T(8,128)(2,1)S(1)}, bf16[3,32,1792]{2,1,0:T(8,128)(2,1)S(1)}, u32[]{:S(2)}, u32[]{:S(2)}) collective-permute-start(bf16[3,32,1792]{2,1,0:T(8,128)(2,1)S(1)} %collective-permute-done.10), channel_id=1, source_target_pairs={{0,8},{8,16},{16,24},{24,0},{1,9},{9,17},{17,25},{25,1},{2,10},{10... | collective-permute-start | bytes 1032200 | tf_op jit(solution)/shard_map/ppermute | solution.py:25
  135.2 0.0 collective-permute-done.12
  135.2 3.1 %collective-permute-start.15 = (bf16[3,32,1792]{2,1,0:T(8,128)(2,1)S(1)}, bf16[3,32,1792]{2,1,0:T(8,128)(2,1)S(1)}, u32[]{:S(2)}, u32[]{:S(2)}) collective-permute-start(bf16[3,32,1792]{2,1,0:T(8,128)(2,1)S(1)} %collective-permute-done.11), channel_id=1, source_target_pairs={{0,24},{8,0},{16,8},{24,16},{1,25},{9,1},{17,9},{25,17},{2,26},{10... | collective-permute-start | bytes 1032200 | tf_op jit(solution)/shard_map/ppermute | solution.py:25
  138.4 3.0 %collective-permute-done.13 = bf16[3,32,1792]{2,1,0:T(8,128)(2,1)S(1)} collective-permute-done((bf16[3,32,1792]{2,1,0:T(8,128)(2,1)S(1)}, bf16[3,32,1792]{2,1,0:T(8,128)(2,1)S(1)}, u32[]{:S(2)}, u32[]{:S(2)}) %collective-permute-start.13) | collective-permute-done | bytes 344096 | tf_op jit(solution)/shard_map/ppermute | solution.py:25
  141.4 0.0 collective-permute-done.16
  141.4 0.0 collective-permute-done.17
  141.4 0.1 collective-permute-done.14
  141.6 0.9 fusion.13
  142.5 3.3 %collective-permute-done.15 = bf16[3,32,1792]{2,1,0:T(8,128)(2,1)S(1)} collective-permute-done((bf16[3,32,1792]{2,1,0:T(8,128)(2,1)S(1)}, bf16[3,32,1792]{2,1,0:T(8,128)(2,1)S(1)}, u32[]{:S(2)}, u32[]{:S(2)}) %collective-permute-start.15) | collective-permute-done | bytes 344096 | tf_op jit(solution)/shard_map/ppermute | solution.py:25
  145.8 0.0 copy-start.1
  145.8 1.5 %copy-done.1 = bf16[3,4,64,1792]{3,2,1,0:T(8,128)(2,1)} copy-done((bf16[3,4,64,1792]{3,2,1,0:T(8,128)(2,1)}, bf16[3,4,64,1792]{3,2,1,0:T(8,128)(2,1)S(1)}, u32[]{:S(2)}) %copy-start.1) | copy-done | bytes 2752536
  (19 shorter events, 0.5 us)
Async XLA Ops:
  0.6 18.4 %copy-start = (bf16[1,1,768,1792]{3,2,1,0:T(8,128)(2,1)S(1)}, bf16[1,1,768,1792]{3,2,1,0:T(8,128)(2,1)}, u32[]{:S(2)}) copy-start(bf16[1,1,768,1792]{3,2,1,0:T(8,128)(2,1)} %param.4) | copy-start | bytes 8257540
  0.6 22.0 %copy-start.2 = (f32[1,64,1792]{2,1,0:T(8,128)S(1)}, f32[1,64,1792]{2,1,0:T(8,128)}, u32[]{:S(2)}) copy-start(f32[1,64,1792]{2,1,0:T(8,128)} %param.5) | copy-start | bytes 1376260
  2.8 16.2 %collective-permute-start.4 = (bf16[3,32,1792]{2,1,0:T(8,128)(2,1)}, bf16[3,32,1792]{2,1,0:T(8,128)(2,1)}, u32[]{:S(2)}, u32[]{:S(2)}) collective-permute-start(bf16[3,32,1792]{2,1,0:T(8,128)(2,1)} %get-tuple-element.22), channel_id=1, source_target_pairs={{0,8},{8,16},{16,24},{24,0},{1,9},{9,17},{17,25},{25,1},{2,10},{10... | collective-permute-start | bytes 1032200 | tf_op jit(solution)/shard_map/ppermute | solution.py:25
  6.2 12.8 %collective-permute-start.5 = (bf16[3,32,1792]{2,1,0:T(8,128)(2,1)}, bf16[3,32,1792]{2,1,0:T(8,128)(2,1)}, u32[]{:S(2)}, u32[]{:S(2)}) collective-permute-start(bf16[3,32,1792]{2,1,0:T(8,128)(2,1)} %get-tuple-element.23), channel_id=1, source_target_pairs={{0,24},{8,0},{16,8},{24,16},{1,25},{9,1},{17,9},{25,17},{2,26},{10... | collective-permute-start | bytes 1032200 | tf_op jit(solution)/shard_map/ppermute | solution.py:25
  11.9 15.5 %collective-permute-start.2 = (bf16[3,32,1792]{2,1,0:T(8,128)(2,1)}, bf16[3,32,1792]{2,1,0:T(8,128)(2,1)}, u32[]{:S(2)}, u32[]{:S(2)}) collective-permute-start(bf16[3,32,1792]{2,1,0:T(8,128)(2,1)} %get-tuple-element.44), channel_id=1, source_target_pairs={{0,8},{8,16},{16,24},{24,0},{1,9},{9,17},{17,25},{25,1},{2,10},{10... | collective-permute-start | bytes 1032200 | tf_op jit(solution)/shard_map/ppermute | solution.py:25
  14.1 13.3 %collective-permute-start.3 = (bf16[3,32,1792]{2,1,0:T(8,128)(2,1)}, bf16[3,32,1792]{2,1,0:T(8,128)(2,1)}, u32[]{:S(2)}, u32[]{:S(2)}) collective-permute-start(bf16[3,32,1792]{2,1,0:T(8,128)(2,1)} %get-tuple-element.43), channel_id=1, source_target_pairs={{0,24},{8,0},{16,8},{24,16},{1,25},{9,1},{17,9},{25,17},{2,26},{10... | collective-permute-start | bytes 1032200 | tf_op jit(solution)/shard_map/ppermute | solution.py:25
  20.3 11.8 %collective-permute-start.6 = (bf16[3,32,1792]{2,1,0:T(8,128)(2,1)S(1)}, bf16[3,32,1792]{2,1,0:T(8,128)(2,1)S(1)}, u32[]{:S(2)}, u32[]{:S(2)}) collective-permute-start(bf16[3,32,1792]{2,1,0:T(8,128)(2,1)S(1)} %get-tuple-element.42), channel_id=1, source_target_pairs={{0,8},{8,16},{16,24},{24,0},{1,9},{9,17},{17,25},{25,1},{2,10},{10... | collective-permute-start | bytes 1032200 | tf_op jit(solution)/shard_map/ppermute | solution.py:25
  22.7 10.6 %collective-permute-start.7 = (bf16[3,32,1792]{2,1,0:T(8,128)(2,1)S(1)}, bf16[3,32,1792]{2,1,0:T(8,128)(2,1)S(1)}, u32[]{:S(2)}, u32[]{:S(2)}) collective-permute-start(bf16[3,32,1792]{2,1,0:T(8,128)(2,1)S(1)} %get-tuple-element.41), channel_id=1, source_target_pairs={{0,24},{8,0},{16,8},{24,16},{1,25},{9,1},{17,9},{25,17},{2,26},{10... | collective-permute-start | bytes 1032200 | tf_op jit(solution)/shard_map/ppermute | solution.py:25
  33.3 8.3 %copy-start.4 = (f32[1,8,1792]{2,1,0:T(8,128)S(1)}, f32[1,8,1792]{2,1,0:T(8,128)}, u32[]{:S(2)}) copy-start(f32[1,8,1792]{2,1,0:T(8,128)} %param.6) | copy-start | bytes 172036
  33.3 8.3 %copy-start.5 = (f32[1,8,1792]{2,1,0:T(8,128)S(1)}, f32[1,8,1792]{2,1,0:T(8,128)}, u32[]{:S(2)}) copy-start(f32[1,8,1792]{2,1,0:T(8,128)} %param.7) | copy-start | bytes 172036
  34.5 27.8 %all-to-all-start = ((bf16[8,3,8,1792]{3,2,1,0:T(8,128)(2,1)}), bf16[8,3,8,1792]{3,2,1,0:T(8,128)(2,1)S(1)}, u32[]{:S(2)}, u32[]{:S(2)}) async-start(bf16[8,3,8,1792]{3,2,1,0:T(8,128)(2,1)} %fusion.3), calls=%async_computation | async-start | bytes 1376256 | tf_op jit(solution)/shard_map/all_to_all | solution.py:105
  41.6 15.8 %collective-permute-start = (f32[8,1792]{1,0:T(8,128)S(1)}, f32[8,1792]{1,0:T(8,128)S(1)}, u32[]{:S(2)}, u32[]{:S(2)}) collective-permute-start(f32[8,1792]{1,0:T(8,128)S(1)} %bitcast.107), channel_id=1, source_target_pairs={{0,32},{32,64},{64,0},{1,33},{33,65},{65,1},{2,34},{34,66},{66,2},... | collective-permute-start | bytes 172040 | tf_op jit(solution)/shard_map/ppermute | solution.py:25
  52.3 10.0 %collective-permute-start.1 = (f32[8,1792]{1,0:T(8,128)S(1)}, f32[8,1792]{1,0:T(8,128)S(1)}, u32[]{:S(2)}, u32[]{:S(2)}) collective-permute-start(f32[8,1792]{1,0:T(8,128)S(1)} %bitcast.108), channel_id=1, source_target_pairs={{0,64},{32,0},{64,32},{1,65},{33,1},{65,33},{2,66},{34,2},{66,34},... | collective-permute-start | bytes 172040 | tf_op jit(solution)/shard_map/ppermute | solution.py:25
  62.5 15.6 %collective-permute-start.8 = (bf16[3,8,1792]{2,1,0:T(8,128)(2,1)S(1)}, bf16[3,8,1792]{2,1,0:T(8,128)(2,1)S(1)}, u32[]{:S(2)}, u32[]{:S(2)}) collective-permute-start(bf16[3,8,1792]{2,1,0:T(8,128)(2,1)S(1)} %reduce_sum.12), channel_id=1, source_target_pairs={{0,32},{32,64},{64,0},{1,33},{33,65},{65,1},{2,34},{34,66},{66,2},... | collective-permute-start | bytes 258056 | tf_op jit(solution)/shard_map/ppermute | solution.py:25
  71.4 10.3 %collective-permute-start.9 = (bf16[3,8,1792]{2,1,0:T(8,128)(2,1)S(1)}, bf16[3,8,1792]{2,1,0:T(8,128)(2,1)S(1)}, u32[]{:S(2)}, u32[]{:S(2)}) collective-permute-start(bf16[3,8,1792]{2,1,0:T(8,128)(2,1)S(1)} %reduce_sum.12), channel_id=1, source_target_pairs={{0,64},{32,0},{64,32},{1,65},{33,1},{65,33},{2,66},{34,2},{66,34},... | collective-permute-start | bytes 258056 | tf_op jit(solution)/shard_map/ppermute | solution.py:25
  82.7 21.2 %all-to-all-start.1 = ((bf16[8,3,8,1792]{3,2,1,0:T(8,128)(2,1)}), bf16[8,3,8,1792]{3,2,1,0:T(8,128)(2,1)S(1)}, u32[]{:S(2)}, u32[]{:S(2)}) async-start(bf16[8,3,8,1792]{3,2,1,0:T(8,128)(2,1)} %broadcast_in_dim.59), calls=%async_computation.1 | async-start | bytes 1376256 | tf_op jit(solution)/shard_map/all_to_all | solution.py:114
  88.2 53.2 %collective-permute-start.16 = (bf16[64,1792]{1,0:T(8,128)(2,1)S(1)}, bf16[64,1792]{1,0:T(8,128)(2,1)S(1)}, u32[]{:S(2)}, u32[]{:S(2)}) collective-permute-start(bf16[64,1792]{1,0:T(8,128)(2,1)S(1)} %get-tuple-element.35), channel_id=1, source_target_pairs={{0,32},{32,64},{64,0},{1,33},{33,65},{65,1},{2,34},{34,66},{66,2},... | collective-permute-start | bytes 688136 | tf_op jit(solution)/shard_map/ppermute | solution.py:25
  92.5 48.9 %collective-permute-start.17 = (bf16[64,1792]{1,0:T(8,128)(2,1)S(1)}, bf16[64,1792]{1,0:T(8,128)(2,1)S(1)}, u32[]{:S(2)}, u32[]{:S(2)}) collective-permute-start(bf16[64,1792]{1,0:T(8,128)(2,1)S(1)} %get-tuple-element.36), channel_id=1, source_target_pairs={{0,64},{32,0},{64,32},{1,65},{33,1},{65,33},{2,66},{34,2},{66,34},... | collective-permute-start | bytes 688136 | tf_op jit(solution)/shard_map/ppermute | solution.py:25
  104.0 27.2 %collective-permute-start.11 = (bf16[3,32,1792]{2,1,0:T(8,128)(2,1)S(1)}, bf16[3,32,1792]{2,1,0:T(8,128)(2,1)S(1)}, u32[]{:S(2)}, u32[]{:S(2)}) collective-permute-start(bf16[3,32,1792]{2,1,0:T(8,128)(2,1)S(1)} %bitcast.104), channel_id=1, source_target_pairs={{0,24},{8,0},{16,8},{24,16},{1,25},{9,1},{17,9},{25,17},{2,26},{10... | collective-permute-start | bytes 1032200 | tf_op jit(solution)/shard_map/ppermute | solution.py:25
  111.7 23.5 %collective-permute-start.12 = (bf16[3,32,1792]{2,1,0:T(8,128)(2,1)S(1)}, bf16[3,32,1792]{2,1,0:T(8,128)(2,1)S(1)}, u32[]{:S(2)}, u32[]{:S(2)}) collective-permute-start(bf16[3,32,1792]{2,1,0:T(8,128)(2,1)S(1)} %bitcast.105), channel_id=1, source_target_pairs={{0,8},{8,16},{16,24},{24,0},{1,9},{9,17},{17,25},{25,1},{2,10},{10... | collective-permute-start | bytes 1032200 | tf_op jit(solution)/shard_map/ppermute | solution.py:25
  113.6 15.6 %collective-permute-start.10 = (bf16[3,32,1792]{2,1,0:T(8,128)(2,1)S(1)}, bf16[3,32,1792]{2,1,0:T(8,128)(2,1)S(1)}, u32[]{:S(2)}, u32[]{:S(2)}) collective-permute-start(bf16[3,32,1792]{2,1,0:T(8,128)(2,1)S(1)} %bitcast.102), channel_id=1, source_target_pairs={{0,8},{8,16},{16,24},{24,0},{1,9},{9,17},{17,25},{25,1},{2,10},{10... | collective-permute-start | bytes 1032200 | tf_op jit(solution)/shard_map/ppermute | solution.py:25
  115.8 25.7 %copy-start.3 = (f32[1,64,1792]{2,1,0:T(8,128)S(1)}, f32[1,64,1792]{2,1,0:T(8,128)}, u32[]{:S(2)}) copy-start(f32[1,64,1792]{2,1,0:T(8,128)} %param.5) | copy-start | bytes 1376260
  129.2 12.1 %collective-permute-start.13 = (bf16[3,32,1792]{2,1,0:T(8,128)(2,1)S(1)}, bf16[3,32,1792]{2,1,0:T(8,128)(2,1)S(1)}, u32[]{:S(2)}, u32[]{:S(2)}) collective-permute-start(bf16[3,32,1792]{2,1,0:T(8,128)(2,1)S(1)} %bitcast.103), channel_id=1, source_target_pairs={{0,24},{8,0},{16,8},{24,16},{1,25},{9,1},{17,9},{25,17},{2,26},{10... | collective-permute-start | bytes 1032200 | tf_op jit(solution)/shard_map/ppermute | solution.py:25
  131.2 10.4 %collective-permute-start.14 = (bf16[3,32,1792]{2,1,0:T(8,128)(2,1)S(1)}, bf16[3,32,1792]{2,1,0:T(8,128)(2,1)S(1)}, u32[]{:S(2)}, u32[]{:S(2)}) collective-permute-start(bf16[3,32,1792]{2,1,0:T(8,128)(2,1)S(1)} %collective-permute-done.10), channel_id=1, source_target_pairs={{0,8},{8,16},{16,24},{24,0},{1,9},{9,17},{17,25},{25,1},{2,10},{10... | collective-permute-start | bytes 1032200 | tf_op jit(solution)/shard_map/ppermute | solution.py:25
  135.2 10.6 %collective-permute-start.15 = (bf16[3,32,1792]{2,1,0:T(8,128)(2,1)S(1)}, bf16[3,32,1792]{2,1,0:T(8,128)(2,1)S(1)}, u32[]{:S(2)}, u32[]{:S(2)}) collective-permute-start(bf16[3,32,1792]{2,1,0:T(8,128)(2,1)S(1)} %collective-permute-done.11), channel_id=1, source_target_pairs={{0,24},{8,0},{16,8},{24,16},{1,25},{9,1},{17,9},{25,17},{2,26},{10... | collective-permute-start | bytes 1032200 | tf_op jit(solution)/shard_map/ppermute | solution.py:25
  145.8 1.5 %copy-start.1 = (bf16[3,4,64,1792]{3,2,1,0:T(8,128)(2,1)}, bf16[3,4,64,1792]{3,2,1,0:T(8,128)(2,1)S(1)}, u32[]{:S(2)}) copy-start(bf16[3,4,64,1792]{3,2,1,0:T(8,128)(2,1)S(1)} %bitcast_dynamic-update-slice_fusion) | copy-start | bytes 8257540
